TPU v7x, 128 devices: a whole 4x4x4 slice. The times are simulated.
128 devices in a mesh: row: 16 (over y, x), col: 8 (over z, core).
Axes of the slice: x: 4, y: 4, z: 4, core: 2. Of those that a mesh axis runs over, the one named last changes fastest.
Arguments:
- coarse_kernel: bfloat16 [16, 16, 256, 256], P('row', 'col'), as said below
- interp_coef: bfloat16 [64, 2, 256, 256], P('col'), may hold values from -0.375 to 0.375
- interp_map: int32 [64, 2], replicated, may hold values from 0 to 15, as said below
- energy: float32 [16384], P(('row', 'col')), may hold values from 1 to 3
- start_vectors: float32 [256, 16384], P(None, ('row', 'col')), may hold values from -6 to 6
Outputs:
- second: float32 [256, 16384], P(None, ('row', 'col'))
- residual: float32 [256, 16384], P(None, ('row', 'col'))
- coeffs: float32 [3, 256], replicated
- kernel: bfloat16 [16384, 16384], P('row', 'col')
Inputs may be any that keep to these rules, and one draw needn't show every extreme that they name: coarse_kernel[a, b] is the transpose of coarse_kernel[b, a], so the kernel is symmetric. interp_map[i, 0] is i // 4; interp_map[i, 1] is interp_map[i, 0] - 1 or interp_map[i, 0] + 1 modulo 16: the first where i % 4 == 0, the second where i % 4 == 3.
All inputs are finite; a program needn't handle non-finite values.
Results may differ from a plain program's by a relative error of at most 0.0052.
Values may be sent and summed in bfloat16 or wider, within the bound.
A program may use at most 64 MiB of HBM per device.

v0:
```python
import jax
import jax.numpy as jnp
from jax import lax
from jax.sharding import PartitionSpec as P

KR = 4


EPS = 1e-06


def spread(value, axis, source):
    kept = jnp.where(lax.axis_index(axis) == source, value, 0).astype(value.dtype)
    return lax.psum(kept, axis)


def extended(cells, sides, width):
    for axis, dim in sides:
        count = lax.axis_size(axis)
        head = lax.slice_in_dim(cells, 0, width, axis=dim)
        tail = lax.slice_in_dim(cells, cells.shape[dim] - width, cells.shape[dim], axis=dim)
        cells = jnp.concatenate(
            [
                lax.ppermute(tail, axis, [(i, (i + 1) % count) for i in range(count)]),
                cells,
                lax.ppermute(head, axis, [((i + 1) % count, i) for i in range(count)]),
            ],
            axis=dim,
        )
    return cells


def right_product(blocks, columns, coefs):
    summed = jnp.zeros(
        (blocks.shape[0], coefs.shape[0], coefs.shape[2], coefs.shape[3]), jnp.float32
    )
    for neighbor in range(coefs.shape[1]):
        picked = jnp.take(blocks, columns[:, neighbor], axis=1)
        summed = summed + jnp.einsum(
            "ajxy,jyz->ajxz", picked, coefs[:, neighbor], preferred_element_type=jnp.float32
        )
    return summed.astype(jnp.bfloat16)


def per_device(coarse_kernel, interp_coef, interp_map, energy, start_vectors):
    rows_count = lax.axis_size("row")
    cols_count = lax.axis_size("col")
    row_index = lax.axis_index("row")
    col_index = lax.axis_index("col")
    col_fine = interp_coef.shape[0]
    bands = interp_coef.shape[2]
    coarse_rows = coarse_kernel.shape[0]
    coarse_cols = coarse_kernel.shape[1]
    coarse_total = coarse_rows * rows_count
    col_maps = lax.dynamic_slice_in_dim(interp_map, col_index * col_fine, col_fine, 0)
    col_local = (col_maps - (col_index * coarse_cols - 1)) % coarse_total
    row_maps = lax.dynamic_slice_in_dim(interp_map, row_index * KR, KR, 0)
    row_local = (row_maps - (row_index * coarse_rows - 1)) % coarse_total
    offset = row_index * KR % col_fine
    own_slice = lax.dynamic_slice_in_dim(interp_coef, offset, KR, 0)
    source = row_index * KR // col_fine
    left_coef = spread(own_slice, "col", source)
    padded = extended(coarse_kernel, (("row", 0), ("col", 1)), 1)
    right_part = right_product(padded, col_local, interp_coef)
    fine_sum = jnp.zeros((KR, col_fine, bands, bands), jnp.float32)
    for neighbor in range(left_coef.shape[1]):
        picked = jnp.take(right_part, row_local[:, neighbor], axis=0)
        fine_sum = fine_sum + jnp.einsum(
            "ixy,ijxz->ijyz", left_coef[:, neighbor], picked, preferred_element_type=jnp.float32
        )
    kernel_tile = jnp.transpose(fine_sum.astype(jnp.bfloat16), (0, 2, 1, 3)).reshape(
        KR * bands, col_fine * bands
    )
    shard_rows = start_vectors.shape[1]
    total_rows = shard_rows * rows_count * cols_count

    def mean_square(vectors):
        return lax.psum(jnp.sum(vectors * vectors, axis=1), ("row", "col")) / total_rows

    def inner_mean(one_side, other_side):
        return lax.psum(jnp.sum(one_side * other_side, axis=1), ("row", "col")) / total_rows

    def fetch_columns(packed):
        gathered = lax.all_gather(packed, ("row", "col"), axis=1, tiled=True)
        wanted = lax.dynamic_slice_in_dim(
            gathered, col_index * col_fine * bands, col_fine * bands, 1
        )
        return wanted

    def apply_operator(vectors):
        packed = vectors.astype(jnp.bfloat16)
        columns = fetch_columns(packed)
        partial_value = lax.dot_general(
            columns, kernel_tile, (((1,), (1,)), ((), ())), preferred_element_type=jnp.float32
        )
        summed = lax.psum_scatter(partial_value, "col", scatter_dimension=1, tiled=True)
        return summed + energy[None, :] * vectors

    scaling = jnp.sqrt(mean_square(start_vectors) + EPS)
    first = start_vectors / scaling[:, None]
    image_one = apply_operator(first)
    alpha_one = inner_mean(first, image_one)
    remain = image_one - alpha_one[:, None] * first
    beta_one = jnp.sqrt(mean_square(remain) + EPS)
    second = remain / beta_one[:, None]
    image_two = apply_operator(second)
    shifted = image_two - beta_one[:, None] * first
    alpha_two = inner_mean(second, shifted)
    residual = shifted - alpha_two[:, None] * second
    return (second, residual, jnp.stack([alpha_one, beta_one, alpha_two]), kernel_tile)


def solution(mesh):
    return jax.shard_map(
        per_device,
        mesh=mesh,
        in_specs=(
            P("row", "col", None, None),
            P("col", None, None, None),
            P(),
            P(("row", "col")),
            P(None, ("row", "col")),
        ),
        out_specs=(P(None, ("row", "col")), P(None, ("row", "col")), P(), P("row", "col")),
        check_vma=False,
    )
```

profile of v0, /device:TPU:1, one launch (start us, length us, event | category | flops | bytes accessed | tf_op | source)
XLA Modules:
  0.0 511.9 jit_solution(13880530808919477990)
XLA Ops:
  8.1 1.4 constant_dynamic-slice_fusion.2
  10.0 1.0 broadcast_select_fusion
  11.2 69.1 %psum.35 = f32[256]{0:T(256)S(1)} all-reduce(f32[256]{0:T(256)S(1)} %multiply_reduce_fusion.3), channel_id=1, replica_groups=mesh['row'=16,'col'=8] {'row','col'}, use_global_device_ids=true, to_apply=%region_1.2 | all-reduce | flops 256 | bytes 2048 | tf_op jit(solution)/shard_map/psum | solution.py:78
  81.5 4.6 collective-permute-start.1
  86.1 5.7 %collective-permute-done = bf16[1,2,256,256]{3,2,1,0:T(8,128)(2,1)S(1)} collective-permute-done((bf16[1,2,256,256]{3,2,1,0:T(8,128)(2,1)S(1)}, bf16[1,2,256,256]{3,2,1,0:T(8,128)(2,1)S(1)}, u32[]{:S(2)}, u32[]{:S(2)}) %collective-permute-start) | collective-permute-done | bytes 262176 | tf_op jit(solution)/shard_map/ppermute | solution.py:24
  92.7 0.8 collective-permute-start.3
  93.7 3.8 collective-permute-done.2
  97.5 2.9 collective-permute-done.3
  100.5 2.4 gather_fusion.1
  102.9 2.5 gather_fusion
  105.4 3.4 fusion.7
  109.3 1.0 fusion.6
  110.4 2.8 gather_fusion.3
  113.2 2.8 gather_fusion.2
  116.0 3.9 fusion
  119.9 1.4 add_convert_fusion
  121.3 2.4 copy.15
  123.8 3.5 copy.23
  127.2 29.0 %all-gather.3.cloned.1.call-done = bf16[256,16384]{1,0:T(8,128)(2,1)} async-done(((bf16[256,128]{1,0:T(8,128)(2,1)}), bf16[256,16384]{1,0:T(8,128)(2,1)}) %all-gather.3.cloned.1.call-update) | async-done | bytes 8388624 | tf_op jit(solution)/shard_map/all_gather | solution.py:84
  156.2 4.9 fusion.29
  161.1 28.9 %reduce-scatter.3.cloned.1.call-done = f32[256,128]{1,0:T(8,128)} async-done(((f32[256,1024]{1,0:T(8,128)}), f32[256,128]{1,0:T(8,128)}) %reduce-scatter.3.cloned.1.call-update) | async-done | bytes 131088 | tf_op jit(solution)/shard_map/reduce_scatter | solution.py:96
  190.1 1.1 multiply_reduce_fusion.2
  191.2 67.6 %psum.37 = f32[256]{0:T(256)S(1)} all-reduce(f32[256]{0:T(256)S(1)} %multiply_reduce_fusion.2), channel_id=1, replica_groups=mesh['row'=16,'col'=8] {'row','col'}, use_global_device_ids=true, to_apply=%region_5.8 | all-reduce | flops 256 | bytes 2048 | tf_op jit(solution)/shard_map/psum | solution.py:81
  258.8 1.1 multiply_reduce_fusion.1
  259.9 62.6 %psum.38 = f32[256]{0:T(256)S(1)} all-reduce(f32[256]{0:T(256)S(1)} %multiply_reduce_fusion.1), channel_id=1, replica_groups=mesh['row'=16,'col'=8] {'row','col'}, use_global_device_ids=true, to_apply=%region_7.10 | all-reduce | flops 256 | bytes 2048 | tf_op jit(solution)/shard_map/psum | solution.py:78
  322.5 1.7 fusion.42
  324.3 75.8 %all-gather.5.cloned.1.call-done = bf16[256,16384]{1,0:T(8,128)(2,1)} async-done(((bf16[256,128]{1,0:T(8,128)(2,1)}), bf16[256,16384]{1,0:T(8,128)(2,1)}) %all-gather.5.cloned.1.call-update) | async-done | bytes 8388624 | tf_op jit(solution)/shard_map/all_gather | solution.py:84
  400.0 4.8 fusion.25
  404.9 29.0 %reduce-scatter.5.cloned.1.call-done = f32[256,128]{1,0:T(8,128)} async-done(((f32[256,1024]{1,0:T(8,128)}), f32[256,128]{1,0:T(8,128)}) %reduce-scatter.5.cloned.1.call-update) | async-done | bytes 131088 | tf_op jit(solution)/shard_map/reduce_scatter | solution.py:96
  433.9 1.1 multiply_reduce_fusion
  435.0 67.4 %psum.39 = f32[256]{0:T(256)S(1)} all-reduce(f32[256]{0:T(256)S(1)} %multiply_reduce_fusion), channel_id=1, replica_groups=mesh['row'=16,'col'=8] {'row','col'}, use_global_device_ids=true, to_apply=%region_10.13 | all-reduce | flops 256 | bytes 2048 | tf_op jit(solution)/shard_map/psum | solution.py:81
  503.1 1.7 multiply_subtract_fusion
  (51 shorter events, 4.4 us)
Async XLA Ops:
  8.0 3.1 copy-start.2
  8.0 73.2 %copy-start.6 = (bf16[1,2,256,256]{3,2,1,0:T(8,128)(2,1)S(1)}, bf16[1,2,256,256]{3,2,1,0:T(8,128)(2,1)}, u32[]{:S(2)}) copy-start(bf16[1,2,256,256]{3,2,1,0:T(8,128)(2,1)} %param.9) | copy-start | bytes 786436
  8.0 78.0 %copy-start.8 = (s32[64,2]{0,1:T(2,128)S(1)}, s32[64,2]{0,1:T(2,128)}, u32[]{:S(2)}) copy-start(s32[64,2]{0,1:T(2,128)} %param.11) | copy-start | bytes 1540
  8.0 107.9 %all-reduce.2.cloned.1.call-start = ((), (), s32[]{:S(2)}) async-start(), calls=%async_computation.3 | async-start | bytes 2097152 | tf_op jit(solution)/shard_map/psum | solution.py:14
  11.1 145.1 %all-gather.3.cloned.1.call-start = ((), (), s32[]{:S(2)}) async-start(), calls=%async_computation.2 | async-start | bytes 8454144 | tf_op jit(solution)/shard_map/all_gather | solution.py:84
  81.1 109.0 %reduce-scatter.3.cloned.1.call-start = ((), (), s32[]{:S(2)}) async-start(), calls=%async_computation.4 | async-start | bytes 1179648 | tf_op jit(solution)/shard_map/reduce_scatter | solution.py:96
  81.2 10.7 %collective-permute-start = (bf16[1,2,256,256]{3,2,1,0:T(8,128)(2,1)S(1)}, bf16[1,2,256,256]{3,2,1,0:T(8,128)(2,1)S(1)}, u32[]{:S(2)}, u32[]{:S(2)}) collective-permute-start(bf16[1,2,256,256]{3,2,1,0:T(8,128)(2,1)S(1)} %copy-done.6), channel_id=1, source_target_pairs={{0,8},{8,16},{16,24},{24,32},{32,40},{40,48},{48,56},{56,64},{64,7... | collective-permute-start | bytes 786440 | tf_op jit(solution)/shard_map/ppermute | solution.py:24
  81.5 10.5 %collective-permute-start.1 = (bf16[1,2,256,256]{3,2,1,0:T(8,128)(2,1)S(1)}, bf16[1,2,256,256]{3,2,1,0:T(8,128)(2,1)S(1)}, u32[]{:S(2)}, u32[]{:S(2)}) collective-permute-start(bf16[1,2,256,256]{3,2,1,0:T(8,128)(2,1)S(1)} %copy-done.6), channel_id=1, source_target_pairs={{8,0},{16,8},{24,16},{32,24},{40,32},{48,40},{56,48},{64,56},{72,6... | collective-permute-start | bytes 786440 | tf_op jit(solution)/shard_map/ppermute | solution.py:26
  92.0 5.4 %collective-permute-start.2 = (bf16[3,1,256,256]{3,2,1,0:T(8,128)(2,1)S(1)}, bf16[3,1,256,256]{3,2,1,0:T(8,128)(2,1)S(1)}, u32[]{:S(2)}, u32[]{:S(2)}) collective-permute-start(bf16[3,1,256,256]{3,2,1,0:T(8,128)(2,1)S(1)} %get-tuple-element.16), channel_id=1, source_target_pairs={{0,1},{1,2},{2,3},{3,4},{4,5},{5,6},{6,7},{7,0},{8,9},{9,10},{10,1... | collective-permute-start | bytes 1179656 | tf_op jit(solution)/shard_map/ppermute | solution.py:24
  92.7 7.6 %collective-permute-start.3 = (bf16[3,1,256,256]{3,2,1,0:T(8,128)(2,1)S(1)}, bf16[3,1,256,256]{3,2,1,0:T(8,128)(2,1)S(1)}, u32[]{:S(2)}, u32[]{:S(2)}) collective-permute-start(bf16[3,1,256,256]{3,2,1,0:T(8,128)(2,1)S(1)} %get-tuple-element.17), channel_id=1, source_target_pairs={{1,0},{2,1},{3,2},{4,3},{5,4},{6,5},{7,6},{0,7},{9,8},{10,9},{11,1... | collective-permute-start | bytes 1179656 | tf_op jit(solution)/shard_map/ppermute | solution.py:26
  105.4 3.4 copy-start.1
  105.4 3.9 copy-start.3
  116.0 3.9 copy-start
  116.0 3.9 copy-start.4
  156.2 33.9 %copy-start.7 = (f32[128]{0:T(128)S(1)}, f32[128]{0:T(128)}, u32[]{:S(2)}) copy-start(f32[128]{0:T(128)} %param.12) | copy-start | bytes 1540
  161.1 239.0 %all-gather.5.cloned.1.call-start = ((), (), s32[]{:S(2)}) async-start(), calls=%async_computation.5 | async-start | bytes 8454144 | tf_op jit(solution)/shard_map/all_gather | solution.py:84
  324.2 178.9 %copy-start.5 = (f32[256,128]{1,0:T(8,128)}, f32[256,128]{1,0:T(8,128)S(1)}, u32[]{:S(2)}) copy-start(f32[256,128]{1,0:T(8,128)S(1)} %get-tuple-element.7) | copy-start | bytes 393220
  324.2 109.7 %reduce-scatter.5.cloned.1.call-start = ((), (), s32[]{:S(2)}) async-start(), calls=%async_computation.6 | async-start | bytes 1179648 | tf_op jit(solution)/shard_map/reduce_scatter | solution.py:96
Sparse Core Ops, SparseCore 0:
  11.2 64.1 all-reduce.1
  161.2 28.8 reduce-scatter.2
  405.0 28.8 reduce-scatter.4
Sparse Core Ops, SparseCore 1:
  81.2 74.9 all-gather.2
  324.3 75.7 all-gather.4
where the time goes:
time: 513 us; the launch traced here: 512 us
  blocking collectives  267 us (52%)
  waiting for transfers between devices  175 us (34%)
  matrix products  19.4 us (4%)
  local copies, waits for them, and re-layouts  19 us (4%)
  between operations  15.4 us (3%)
  other arithmetic  9.65 us (2%)
  starting transfers between devices  6.59 us (1%)
    psum x2, blocking collectives, inner_mean(): lax.psum(jnp.sum(one_side * other_side, axis=1), ('row', 'col'))  135 us
    psum x2, blocking collectives, mean_square(): lax.psum(jnp.sum(vectors * vectors, axis=1), ('row', 'col')) / total_rows  132 us
    all_gather x2, waiting for transfers between devices, fetch_columns(): gathered = lax.all_gather(packed, ('row', 'col'), axis=1, tiled=True)  105 us
    reduce_scatter x2, waiting for transfers between devices, apply_operator(): lax.psum_scatter(partial_value, 'col', scatter_dimension=1, tiled=True)  57.9 us
  transfers between devices with their start and end apart: 9, of which 7 were waited for; matrix products, arithmetic and copies ran while one was open for 5% of the time, Pallas kernels for 0%

commit v1 on v0

v1 whole, which is shorter than its diff:
```python
import jax
import jax.numpy as jnp
from jax import lax
from jax.experimental import pallas as pl
from jax.experimental.pallas import tpu as pltpu
from jax.sharding import PartitionSpec as P

ROWS = 16
COLS = 8
BANDS = 256
NVEC = 256
FINE = 8
KR = 4
VS = NVEC // ROWS
HALF = 128
ORDER = 16384
EPS = 1e-06
PRESCALE = 0.125
SHIFT = 2.0

F32 = jnp.float32
BF16 = jnp.bfloat16
MESH = pl.DeviceIdType.MESH

NT = (((1,), (1,)), ((), ()))
NN = (((1,), (0,)), ((), ()))


def mm(a, b, dims):
    return lax.dot_general(a, b, dims, preferred_element_type=F32)


def wait_bytes(ref, sem):
    pltpu.make_async_copy(ref, ref, sem).wait()


def kernel(
    map_ref, kc_ref, coef_ref, e_ref, s_ref,
    second_ref, resid_ref, coeffs_ref, tile_ref,
    scol, ecol, gcol, kbuf, ci, cit, lbuf, tbuf,
    hw_send, hw_recv, wsend, wfull, usend, ured, hu_send, hu_recv,
    zs_send, zs_recv, sec_send, sec_nat, sh_send, sh_nat, cf_send, cf_recv,
    ssem, rsem, tsem,
):
    r = lax.axis_index("row")
    c = lax.axis_index("col")
    z = lax.div(c, 2)
    k = lax.rem(c, 2)
    x = lax.rem(r, 4)
    y = lax.div(r, 4)
    diag_col = lax.div(r, 2)
    is_diag = c == diag_col
    c_prev = lax.rem(c + COLS - 1, COLS)
    c_next = lax.rem(c + 1, COLS)
    finish = []

    def remote(src, dst, sem, tr, tc):
        pltpu.make_async_remote_copy(
            src_ref=src, dst_ref=dst, send_sem=ssem.at[sem], recv_sem=rsem.at[sem],
            device_id=(tr, tc), device_id_type=MESH,
        ).start()

    def local(src, dst, sem):
        pltpu.make_async_copy(src, dst, rsem.at[sem]).start()

    def maybe_self(src, dst, sem, tr, tc):
        @pl.when(is_diag)
        def _():
            local(src, dst, sem)

        @pl.when(jnp.logical_not(is_diag))
        def _():
            remote(src, dst, sem, tr, tc)

    def finish_diag(sem, buf):
        def run():
            @pl.when(is_diag)
            def _():
                wait_bytes(buf.at[pl.ds(0, 15)], ssem.at[sem])

            @pl.when(jnp.logical_not(is_diag))
            def _():
                wait_bytes(buf, ssem.at[sem])

        finish.append(run)

    def finish_plain(sem, buf):
        finish.append(lambda: wait_bytes(buf, ssem.at[sem]))

    S, E, KH, CA, CB = 0, 1, 2, 3, 4
    base = 5

    for t in range(ROWS):
        tr = lax.rem(r + t, ROWS)
        src = s_ref.at[pl.ds(pl.multiple_of(tr * VS, VS), VS), :]
        dst = scol.at[lax.rem(r, 2) * COLS + c]
        (maybe_self if t == 0 else remote)(src, dst, S, tr, diag_col)
    finish_diag(S, scol)
    for t in range(ROWS):
        tr = lax.rem(r + t, ROWS)
        dst = ecol.at[lax.rem(r, 2) * COLS + c]
        (maybe_self if t == 0 else remote)(e_ref, dst, E, tr, diag_col)
    finish_diag(E, ecol)

    serves = lax.div(x, 2) == k
    delta = lax.rem(y - z + 4, 4)
    mine = lax.rem(x, 2) * KR + delta
    for t in range(1, 4):
        tz = lax.rem(z + t, 4)

        @pl.when(serves)
        def _(tz=tz):
            remote(coef_ref.at[mine], ci.at[delta], CA, 4 * z + x, 2 * tz + lax.div(delta, 2))

    for dr in (1, ROWS - 1):
        tr = lax.rem(r + dr, ROWS)
        slot = 0 if dr == 1 else 2
        remote(kc_ref.at[0], kbuf.at[pl.ds(4 * slot + 1, 2)], KH, tr, c)
    for dr in (0, 1, ROWS - 1):
        tr = lax.rem(r + dr, ROWS)
        slot = {0: 1, 1: 0, ROWS - 1: 2}[dr]
        remote(kc_ref.at[0, 0], kbuf.at[4 * slot + 3], KH, tr, c_prev)
        remote(kc_ref.at[0, 1], kbuf.at[4 * slot], KH, tr, c_next)
    for b in range(2):
        kbuf[5 + b] = kc_ref[0, b]
    finish_plain(KH, kbuf.at[pl.ds(0, 10)])

    plus = []
    for j in range(FINE):
        home = c * 2 + j // KR
        flag = map_ref[c * FINE + j, 1] == lax.rem(home + 1, ROWS)
        plus.append(flag.astype(F32))

    def restrict(parts, app):
        acc = [jnp.zeros((VS, BANDS), F32) for _ in range(4)]
        for j in range(FINE):
            home = 1 + j // KR
            own = parts[j].astype(BF16)
            up = parts[j] * plus[j]
            both = jnp.concatenate([parts[j] - up, up], axis=0).astype(BF16)
            acc[home] = acc[home] + mm(own, coef_ref[j, 0], NT)
            side = mm(both, coef_ref[j, 1], NT)
            acc[home - 1] = acc[home - 1] + side[:VS]
            acc[home + 1] = acc[home + 1] + side[VS:]
        sem = base + 8 * app
        hw_send[app, 0] = acc[0].astype(BF16)
        hw_send[app, 1] = acc[3].astype(BF16)
        remote(hw_send.at[app, 0], hw_recv.at[app, 1], sem, r, c_prev)
        remote(hw_send.at[app, 1], hw_recv.at[app, 0], sem, r, c_next)
        finish_plain(sem, hw_send.at[app])
        wait_bytes(hw_recv.at[app], rsem.at[sem])
        w0 = acc[1] + hw_recv[app, 0].astype(F32)
        w1 = acc[2] + hw_recv[app, 1].astype(F32)
        wsend[app] = jnp.concatenate([w0, w1], axis=1).astype(BF16)

    def gather_plane(app):
        sem = base + 8 * app + 1
        local(wsend.at[app], wfull.at[app, r], sem)
        for t in range(1, ROWS):
            remote(wsend.at[app], wfull.at[app, r], sem, lax.rem(r + t, ROWS), c)
        finish_plain(sem, wfull.at[app, pl.ds(0, 15)])

    def coarse_apply(app):
        wait_bytes(wfull.at[app], rsem.at[base + 8 * app + 1])
        full = wfull[app].reshape(NVEC, 2 * BANDS)
        part = mm(full[:, :BANDS], kc_ref[0, 0], NT) + mm(full[:, BANDS:], kc_ref[0, 1], NT)
        usend[app] = part.astype(BF16).reshape(ROWS, VS, BANDS)
        sem = base + 8 * app + 2
        for t in range(ROWS):
            tr = lax.rem(r + t, ROWS)
            dst = ured.at[app, lax.rem(r, 2) * COLS + c]
            (maybe_self if t == 0 else remote)(usend.at[app, tr], dst, sem, tr, diag_col)
        finish_diag(sem, usend.at[app])

    def reduce_coarse(app):
        wait_bytes(ured.at[app], rsem.at[base + 8 * app + 2])
        u = []
        for h in range(2):
            total = ured[app, h * COLS].astype(F32)
            for t in range(1, COLS):
                total = total + ured[app, h * COLS + t].astype(F32)
            u.append(total)
        sem = base + 8 * app + 3
        for h in range(2):
            hu_send[app, h] = u[h].astype(BF16)
        remote(hu_send.at[app, 0], hu_recv.at[app, 1], sem, r, c_prev)
        remote(hu_send.at[app, 1], hu_recv.at[app, 0], sem, r, c_next)
        finish_plain(sem, hu_send.at[app])
        wait_bytes(hu_recv.at[app], rsem.at[sem])
        return [hu_recv[app, 0].astype(F32), u[0], u[1], hu_recv[app, 1].astype(F32)]

    def prolong(u, j):
        home = 1 + j // KR
        side = u[home - 1] * (1.0 - plus[j]) + u[home + 1] * plus[j]
        return mm(u[home].astype(BF16), coef_ref[j, 0], NN) + mm(side.astype(BF16), coef_ref[j, 1], NN)

    def exchange_sums(app, message):
        sem = base + 8 * app + 4
        zs_send[app] = message
        local(zs_send.at[app], zs_recv.at[app, c], sem)
        for t in range(1, COLS):
            remote(zs_send.at[app], zs_recv.at[app, c], sem, r, lax.rem(c + t, COLS))
        finish_plain(sem, zs_recv.at[app, pl.ds(0, 7)])

    def sums(app):
        wait_bytes(zs_recv.at[app], rsem.at[base + 8 * app + 4])
        total = zs_recv[app, 0]
        for t in range(1, COLS):
            total = total + zs_recv[app, t]
        return total

    def to_native(src, dst, sem):
        start = lax.rem(r, 2) * COLS + c
        for t in range(ROWS):
            q = lax.rem(start + t, ROWS)
            tr = 2 * c + lax.div(q, COLS)
            tc = lax.rem(q, COLS)
            (maybe_self if t == 0 else remote)(src.at[q], dst.at[r], sem, tr, tc)
        finish_diag(sem, src)

    lanes = lax.broadcasted_iota(jnp.int32, (VS, HALF), 1)

    def s_block(j):
        return jnp.concatenate([scol[2 * j], scol[2 * j + 1]], axis=1) * PRESCALE

    def d_block(j):
        return jnp.concatenate([ecol[2 * j], ecol[2 * j + 1]], axis=1) - SHIFT

    def row_sum(v):
        return jnp.sum(v, axis=1, keepdims=True)

    wait_bytes(scol, rsem.at[S])
    restrict([s_block(j) for j in range(FINE)], 0)
    gather_plane(0)

    sibling = 2 * z + (1 - k)
    at_source = z == y
    home_core = lax.div(x, 2)
    local_at = lax.rem(x, 2) * KR

    @pl.when(jnp.logical_not(at_source))
    def _():
        mine_pair = ci.at[pl.ds(2 * k, 2)]
        wait_bytes(mine_pair, rsem.at[CA])
        remote(mine_pair, mine_pair, CB, r, sibling)

    @pl.when(jnp.logical_and(at_source, k == home_core))
    def _():
        pltpu.make_async_copy(coef_ref.at[pl.ds(local_at, KR)], ci, rsem.at[CA]).start()
        remote(coef_ref.at[pl.ds(local_at, KR)], ci, CB, r, sibling)
        wait_bytes(ci, rsem.at[CA])

    coarse_apply(0)

    @pl.when(jnp.logical_not(at_source))
    def _():
        wait_bytes(ci.at[pl.ds(0, 2)], rsem.at[CB])

    @pl.when(jnp.logical_and(at_source, k != home_core))
    def _():
        wait_bytes(ci, rsem.at[CB])

    wait_bytes(kbuf.at[pl.ds(0, 10)], rsem.at[KH])
    for i in range(KR):
        for n in range(2):
            cit[i, n] = ci[i, n].T

    up_row = []
    for i in range(KR):
        flag = map_ref[r * KR + i, 1] == lax.rem(r + 1, ROWS)
        up_row.append(jnp.where(flag, 8, 0))
    for i in range(KR):
        for b in range(4):
            value = mm(cit[i, 0], kbuf[4 + b], NN) + mm(cit[i, 1], kbuf[up_row[i] + b], NN)
            lbuf[b, pl.ds(i * BANDS, BANDS), :] = value.astype(BF16)

    def tile_piece(j):
        home = 1 + j // KR
        flag = map_ref[c * FINE + j, 1] == lax.rem(c * 2 + j // KR + 1, ROWS)
        other = jnp.where(flag, home + 1, home - 1)
        for m in range(KR):
            rows = pl.ds(m * BANDS, BANDS)
            value = mm(lbuf[home, rows], coef_ref[j, 0], NN) + mm(lbuf[other, rows], coef_ref[j, 1], NN)
            tbuf[j, rows, :] = value.astype(BF16)
        pltpu.make_async_copy(
            tbuf.at[j], tile_ref.at[:, pl.ds(j * BANDS, BANDS)], tsem.at[j]
        ).start()

    u = reduce_coarse(0)
    wait_bytes(ecol, rsem.at[E])
    parts = []
    ss = sg = gg = jnp.zeros((VS, 1), F32)
    for j in range(FINE):
        s_j = s_block(j)
        g_j = prolong(u, j) + d_block(j) * s_j
        gcol[j] = g_j
        parts.append(g_j)
        ss = ss + row_sum(s_j * s_j)
        sg = sg + row_sum(s_j * g_j)
        gg = gg + row_sum(g_j * g_j)
    restrict(parts, 1)
    gather_plane(1)
    exchange_sums(0, jnp.where(lanes == 0, ss, jnp.where(lanes == 1, sg, gg)))
    for j in range(4):
        tile_piece(j)
    coarse_apply(1)

    mean = sums(0) / ORDER
    ss, sg, gg = mean[:, 0:1], mean[:, 1:2], mean[:, 2:3]
    var = ss + EPS * PRESCALE * PRESCALE
    scale = jnp.sqrt(var)
    alpha_one = (sg + SHIFT * ss) / var
    mix = SHIFT - alpha_one
    remain_sq = (gg + 2.0 * mix * sg + mix * mix * ss) / var
    beta = jnp.sqrt(jnp.maximum(remain_sq, 0.0) + EPS)
    inv = 1.0 / (scale * beta)
    for j in range(FINE):
        sec = (gcol[j] + mix * s_block(j)) * inv
        for h in range(2):
            sec_send[2 * j + h] = sec[:, h * HALF:(h + 1) * HALF]
    to_native(sec_send, sec_nat, base + 5)
    for j in range(4, FINE):
        tile_piece(j)

    u = reduce_coarse(1)
    over = beta / scale
    dot = jnp.zeros((VS, 1), F32)
    for j in range(FINE):
        s_j = s_block(j)
        g_j = gcol[j]
        h_j = prolong(u, j) + d_block(j) * g_j
        sec = jnp.concatenate([sec_send[2 * j], sec_send[2 * j + 1]], axis=1)
        shifted = (h_j + mix * g_j) * inv + SHIFT * sec - over * s_j
        dot = dot + row_sum(sec * shifted)
        for h in range(2):
            sh_send[2 * j + h] = shifted[:, h * HALF:(h + 1) * HALF]
    exchange_sums(1, jnp.broadcast_to(dot, (VS, HALF)))
    to_native(sh_send, sh_nat, base + 6)

    alpha_two = sums(1) / ORDER
    cf_send[...] = jnp.where(lanes == 0, alpha_one, jnp.where(lanes == 1, beta, alpha_two))
    sem = base + 7
    local(cf_send, cf_recv.at[r], sem)
    for t in range(1, ROWS):
        remote(cf_send, cf_recv.at[r], sem, lax.rem(r + t, ROWS), c)
    finish_plain(sem, cf_recv.at[pl.ds(0, 15)])

    wait_bytes(sec_nat, rsem.at[base + 5])
    sec = sec_nat[...].reshape(NVEC, HALF)
    second_ref[...] = sec
    wait_bytes(sh_nat, rsem.at[base + 6])
    wait_bytes(cf_recv, rsem.at[base + 7])
    coefs = cf_recv[...].reshape(NVEC, HALF)
    resid_ref[...] = sh_nat[...].reshape(NVEC, HALF) - coefs[:, 2:3] * sec
    coeffs_ref[...] = coefs.T[0:8]

    for j in range(FINE):
        pltpu.make_async_copy(
            tbuf.at[j], tile_ref.at[:, pl.ds(j * BANDS, BANDS)], tsem.at[j]
        ).wait()

    @pl.when(serves)
    def _():
        wait_bytes(coef_ref.at[pl.ds(0, 3)], ssem.at[CA])

    @pl.when(jnp.logical_not(at_source))
    def _():
        wait_bytes(ci.at[pl.ds(0, 2)], ssem.at[CB])

    @pl.when(jnp.logical_and(at_source, k == home_core))
    def _():
        wait_bytes(ci, ssem.at[CB])

    for run in finish:
        run()


def per_device(coarse_kernel, interp_coef, interp_map, energy, start_vectors):
    vmem = pl.BlockSpec(memory_space=pltpu.VMEM)
    nsem = 5 + 16
    second, residual, coeffs, tile = pl.pallas_call(
        kernel,
        out_shape=(
            jax.ShapeDtypeStruct((NVEC, HALF), F32),
            jax.ShapeDtypeStruct((NVEC, HALF), F32),
            jax.ShapeDtypeStruct((8, NVEC), F32),
            jax.ShapeDtypeStruct((KR * BANDS, FINE * BANDS), BF16),
        ),
        in_specs=[pl.BlockSpec(memory_space=pltpu.SMEM), vmem, vmem, vmem, vmem],
        out_specs=(vmem, vmem, vmem, pl.BlockSpec(memory_space=pl.ANY)),
        scratch_shapes=[
            pltpu.VMEM((16, VS, HALF), F32),
            pltpu.VMEM((16, 1, HALF), F32),
            pltpu.VMEM((FINE, VS, BANDS), F32),
            pltpu.VMEM((12, BANDS, BANDS), BF16),
            pltpu.VMEM((KR, 2, BANDS, BANDS), BF16),
            pltpu.VMEM((KR, 2, BANDS, BANDS), BF16),
            pltpu.VMEM((4, KR * BANDS, BANDS), BF16),
            pltpu.VMEM((FINE, KR * BANDS, BANDS), BF16),
            pltpu.VMEM((2, 2, VS, BANDS), BF16),
            pltpu.VMEM((2, 2, VS, BANDS), BF16),
            pltpu.VMEM((2, VS, 2 * BANDS), BF16),
            pltpu.VMEM((2, ROWS, VS, 2 * BANDS), BF16),
            pltpu.VMEM((2, ROWS, VS, BANDS), BF16),
            pltpu.VMEM((2, 16, VS, BANDS), BF16),
            pltpu.VMEM((2, 2, VS, BANDS), BF16),
            pltpu.VMEM((2, 2, VS, BANDS), BF16),
            pltpu.VMEM((2, VS, HALF), F32),
            pltpu.VMEM((2, COLS, VS, HALF), F32),
            pltpu.VMEM((16, VS, HALF), F32),
            pltpu.VMEM((16, VS, HALF), F32),
            pltpu.VMEM((16, VS, HALF), F32),
            pltpu.VMEM((16, VS, HALF), F32),
            pltpu.VMEM((VS, HALF), F32),
            pltpu.VMEM((16, VS, HALF), F32),
            pltpu.SemaphoreType.DMA((nsem,)),
            pltpu.SemaphoreType.DMA((nsem,)),
            pltpu.SemaphoreType.DMA((FINE,)),
        ],
        compiler_params=pltpu.CompilerParams(
            has_side_effects=True, vmem_limit_bytes=40 * 1024 * 1024
        ),
    )(interp_map, coarse_kernel, interp_coef, energy.reshape(1, HALF), start_vectors)
    return second, residual, coeffs[:3], tile


def solution(mesh):
    return jax.shard_map(
        per_device,
        mesh=mesh,
        in_specs=(
            P("row", "col", None, None),
            P("col", None, None, None),
            P(),
            P(("row", "col")),
            P(None, ("row", "col")),
        ),
        out_specs=(P(None, ("row", "col")), P(None, ("row", "col")), P(), P("row", "col")),
        check_vma=False,
    )
```

time: 513 us -> 102 us (0.20)
  blocking collectives: 267 us -> 0 us
  waiting for transfers between devices: 175 us -> 0 us
  Pallas kernels: 0 us -> 91.9 us
  matrix products: 19.4 us -> 0 us
  between operations: 15.4 us -> 0.64 us
  local copies, waits for them, and re-layouts: 19 us -> 8.78 us
  other arithmetic: 9.65 us -> 0 us
  starting transfers between devices: 6.59 us -> 0 us
    psum x4 -> x0, blocking collectives: 267 us -> none  [the longest x2 135 us: inner_mean(): lax.psum(jnp.sum(one_side * other_side, axis=1), ('row', 'col'))]
    all_gather x2 -> x0, waiting for transfers between devices: 105 us -> none  [fetch_columns(): gathered = lax.all_gather(packed, ('row', 'col'), axis=1, tiled=True)]
    pallas_call x0 -> x1, Pallas kernels: none -> 91.9 us  [per_device(): pl.pallas_call(kernel, out_shape=(jax.ShapeDtypeStruct((NVEC, HALF), F32)...]
    reduce_scatter x2 -> x0, waiting for transfers between devices: 57.9 us -> none  [apply_operator(): lax.psum_scatter(partial_value, 'col', scatter_dimension=1, tiled=True)]
    dot_general x6 -> x0, matrix products: 19.4 us -> none  [the longest x2 9.7 us: apply_operator(): lax.dot_general(columns, kernel_tile, (((1,), (1,)), ((), ())), preferred...]
    ppermute x4 -> x0, waiting for transfers between devices: 12.4 us -> none  [the longest x2 9.52 us: extended(): lax.ppermute(tail, axis, [(i, (i + 1) % count) for i in range(count)])]
    gather x4 -> x0, local copies, waits for them, and re-layouts: 10.5 us -> none  [the longest x2 5.6 us: per_device(): picked = jnp.take(right_part, row_local[:, neighbor], axis=0)]
    ppermute x4 -> x0, starting transfers between devices: 6.39 us -> none  [the longest x2 5.39 us: extended(): lax.ppermute(head, axis, [((i + 1) % count, i) for i in range(count)])]
  transfers between devices with their start and end apart: 9 -> 0, of which waited for: 7 -> 0; matrix products, arithmetic and copies ran while one was open for 5% -> 0% of each run, Pallas kernels for 0% -> 0%
where the time goes in v1:
time: 102 us; the launch traced here: 101 us
  Pallas kernels  91.9 us (90%)
  local copies, waits for them, and re-layouts  8.78 us (9%)
    pallas_call x1, Pallas kernels, per_device(): pl.pallas_call(kernel, out_shape=(jax.ShapeDtypeStruct((NVEC, HALF), F32)...  91.9 us
    unnamed x12, local copies, waits for them, and re-layouts  8.19 us

profile of v1, /device:TPU:1, one launch (start us, length us, event | category | flops | bytes accessed | tf_op | source)
XLA Modules:
  0.0 101.3 jit_solution(13400449699444085828)
XLA Ops:
  0.6 0.8 copy.9.map_ref
  1.4 0.0 copy-start
  1.4 1.6 %copy-done = bf16[8,2,256,256]{3,2,1,0:T(8,128)(2,1)S(1)} copy-done((bf16[8,2,256,256]{3,2,1,0:T(8,128)(2,1)S(1)}, bf16[8,2,256,256]{3,2,1,0:T(8,128)(2,1)}, u32[]{:S(2)}) %copy-start) | copy-done | bytes 2097176
  3.0 0.0 copy-start.1
  3.0 0.9 copy-done.1
  3.9 0.0 copy-start.2
  3.9 0.9 copy-done.2
  4.8 0.0 copy-start.3
  4.8 0.7 copy-done.3
  5.5 91.9 %shard_map.84 = (f32[256,128]{1,0:T(8,128)S(1)}, f32[256,128]{1,0:T(8,128)S(1)}, f32[8,256]{1,0:T(8,128)S(1)}, bf16[1024,2048]{1,0:T(8,128)(2,1)S(1)}) custom-call(s32[64,2]{1,0:T(8,128)S(1)} %copy.9.map_ref, bf16[1,2,256,256]{3,2,1,0:T(8,128)(2,1)S(1)} %copy-done.1, bf16[8,2,256,256]{3,2,1,0:T(8,128)(2,1)S(1)} %copy-done, f32[1,128]{1,0:T(1,128)S(1)} %bitcast.1, ...), custom_call_target="tpu_custom_call" | custom-call | tf_op jit(solution)/shard_map/pallas_call | solution.py:381
  97.4 0.6 slice.3
  98.0 0.7 copy.13
  98.7 0.7 copy.14
  99.3 2.0 %copy.15 = bf16[1024,2048]{1,0:T(8,128)(2,1)} copy(bf16[1024,2048]{1,0:T(8,128)(2,1)S(1)} %get-tuple-element.19) | data formatting | bytes 8388608
Async XLA Ops:
  1.4 1.6 %copy-start = (bf16[8,2,256,256]{3,2,1,0:T(8,128)(2,1)S(1)}, bf16[8,2,256,256]{3,2,1,0:T(8,128)(2,1)}, u32[]{:S(2)}) copy-start(bf16[8,2,256,256]{3,2,1,0:T(8,128)(2,1)} %coef_ref.1) | copy-start | bytes 6291460
  3.0 0.9 copy-start.1
  3.9 0.9 copy-start.2
  4.8 0.7 copy-start.3

commit v2 on v1

v2 whole, which is shorter than its diff:
```python
import jax
import jax.numpy as jnp
from jax import lax
from jax.experimental import pallas as pl
from jax.experimental.pallas import tpu as pltpu
from jax.sharding import PartitionSpec as P

ROWS = 16
COLS = 8
BANDS = 256
NVEC = 256
FINE = 8
KR = 4
VS = NVEC // ROWS
HALF = 128
ORDER = 16384
EPS = 1e-06
PRESCALE = 0.125
SHIFT = 2.0

F32 = jnp.float32
BF16 = jnp.bfloat16
MESH = pl.DeviceIdType.MESH

NT = (((1,), (1,)), ((), ()))
NN = (((1,), (0,)), ((), ()))

OFFSETS = sorted(
    ((dy, dx) for dy in range(4) for dx in range(4)),
    key=lambda t: -(min(t[0], 4 - t[0]) + min(t[1], 4 - t[1])),
)
AROUND = (4, 2, 6, 3, 5, 1, 7, 0)


def mm(a, b, dims):
    return lax.dot_general(a, b, dims, preferred_element_type=F32)


def wait_bytes(ref, sem):
    pltpu.make_async_copy(ref, ref, sem).wait()


def kernel(
    map_ref, kc_hbm, coef_hbm, e_hbm, s_hbm,
    second_ref, resid_ref, coeffs_ref, tile_ref,
    kc_ref, coef_ref, e_ref, s_ref,
    scol, ecol, gcol, kbuf, ci, cit, lbuf, tbuf,
    wsend, wside, wfull, wlow, whigh, usend, ured,
    zs_send, zs_recv, ab_send, ab_recv, sec_send, sec_nat, sh_send, sh_nat, dot_send, dot_recv,
    ssem, rsem, tsem, lsem,
):
    r = lax.axis_index("row")
    c = lax.axis_index("col")
    z = lax.div(c, 2)
    k = lax.rem(c, 2)
    x = lax.rem(r, 4)
    y = lax.div(r, 4)
    odd = lax.rem(r, 2)
    c_prev = lax.rem(c + COLS - 1, COLS)
    c_next = lax.rem(c + 1, COLS)
    diag_col = lax.div(r, 2)
    near_col = lax.rem(diag_col + COLS - 1 + 2 * odd, COLS)
    is_diag = c == diag_col
    is_near = c == near_col
    first_row = 2 * c
    sibling = 2 * z + (1 - k)
    finish = []

    loads = []
    for n, (src, dst) in enumerate(((s_hbm, s_ref), (e_hbm, e_ref), (kc_hbm, kc_ref), (coef_hbm, coef_ref))):
        loads.append(pltpu.make_async_copy(src, dst, lsem.at[n]))
        loads[-1].start()

    barrier = pltpu.get_barrier_semaphore()

    def greet(tr, tc):
        pl.semaphore_signal(barrier, inc=1, device_id=(tr, tc), device_id_type=MESH)

    def plane_row(t):
        dy, dx = t
        return 4 * lax.rem(y + dy, 4) + lax.rem(x + dx, 4)

    for tz in AROUND:
        for t in OFFSETS:
            if tz or t != (0, 0):
                greet(plane_row(t), lax.rem(c + tz, COLS))
    pl.semaphore_wait(barrier, ROWS * COLS - 1)

    def remote(src, dst, sem, tr, tc):
        pltpu.make_async_remote_copy(
            src_ref=src, dst_ref=dst, send_sem=ssem.at[sem], recv_sem=rsem.at[sem],
            device_id=(tr, tc), device_id_type=MESH,
        ).start()

    def local(src, dst, sem):
        pltpu.make_async_copy(src, dst, rsem.at[sem]).start()

    def either(here, src, dst, sem, tr, tc):
        @pl.when(here)
        def _():
            local(src, dst, sem)

        @pl.when(jnp.logical_not(here))
        def _():
            remote(src, dst, sem, tr, tc)

    def finish_plain(sem, buf):
        finish.append(lambda: wait_bytes(buf, ssem.at[sem]))

    def finish_but_one(here, sem, buf, count):
        def run():
            @pl.when(here)
            def _():
                wait_bytes(buf.at[pl.ds(0, count - 1)], ssem.at[sem])

            @pl.when(jnp.logical_not(here))
            def _():
                wait_bytes(buf.at[pl.ds(0, count)], ssem.at[sem])

        finish.append(run)

    S, E, K1, K2, CA, CR, CB, AB, SEC, SH, DOT, ZS, APP = range(13)

    loads[0].wait()
    loads[1].wait()
    for t in OFFSETS:
        tr = plane_row(t)
        src = s_ref.at[pl.ds(pl.multiple_of(tr * VS, VS), VS), :]
        dst = scol.at[odd * COLS + c]
        if t == (0, 0):
            either(is_diag, src, dst, S, tr, diag_col)
        else:
            remote(src, dst, S, tr, diag_col)
    finish_but_one(is_diag, S, scol, ROWS)
    for t in OFFSETS:
        tr = plane_row(t)
        dst = ecol.at[odd * COLS + c]
        if t == (0, 0):
            either(is_diag, e_ref, dst, E, tr, diag_col)
        else:
            remote(e_ref, dst, E, tr, diag_col)
    finish_but_one(is_diag, E, ecol, ROWS)
    loads[2].wait()
    loads[3].wait()

    serves = lax.div(x, 2) == k
    delta = lax.rem(y - z + 4, 4)
    mine = lax.rem(x, 2) * KR + delta
    away = lax.rem(z - y + 4, 4)
    at_source = away == 0
    home_core = lax.div(x, 2)
    is_home = jnp.logical_and(at_source, k == home_core)
    direct = jnp.logical_or(away == 1, away == 3)
    r_next = lax.rem(r + 1, ROWS)
    r_prev = lax.rem(r + ROWS - 1, ROWS)
    pair = pl.ds(2 * k, 2)

    def bulk_direct(b):
        remote(kc_ref.at[0, b], kbuf.at[1 + b], K1, r_next, c)
        remote(kc_ref.at[0, b], kbuf.at[9 + b], K1, r_prev, c)

        @pl.when(serves)
        def _():
            for t in (1, 3):
                remote(
                    coef_ref.at[mine, b], ci.at[delta, b], CA,
                    4 * z + x, 2 * lax.rem(z + t, 4) + lax.div(delta, 2),
                )

    def bulk_second():
        wait_bytes(kbuf.at[pl.ds(0, 4)], rsem.at[K1])
        for slot in range(3):
            remote(kbuf.at[4 * slot + 1], kbuf.at[4 * slot + 3], K2, r, c_prev)
            remote(kbuf.at[4 * slot + 2], kbuf.at[4 * slot], K2, r, c_next)

        @pl.when(direct)
        def _():
            wait_bytes(ci.at[pl.ds(0, 2)], rsem.at[CA])

        @pl.when(away == 1)
        def _():
            remote(ci.at[pair, 0], ci.at[pair, 0], CR, r, 2 * lax.rem(z + 1, 4) + k)

        @pl.when(away == 3)
        def _():
            remote(ci.at[pair, 1], ci.at[pair, 1], CR, r, 2 * lax.rem(z + 3, 4) + k)

    def bulk_siblings():
        @pl.when(away == 2)
        def _():
            wait_bytes(ci.at[pl.ds(0, 2)], rsem.at[CR])

        @pl.when(jnp.logical_not(at_source))
        def _():
            remote(ci.at[pair], ci.at[pair], CB, r, sibling)

        @pl.when(is_home)
        def _():
            src = coef_ref.at[pl.ds(odd * KR, KR)]
            local(src, ci, CA)
            remote(src, ci, CB, r, sibling)

    def bulk_wait():
        @pl.when(is_home)
        def _():
            wait_bytes(ci, rsem.at[CA])

        @pl.when(jnp.logical_not(at_source))
        def _():
            wait_bytes(ci.at[pl.ds(0, 2)], rsem.at[CB])

        @pl.when(jnp.logical_and(at_source, k != home_core))
        def _():
            wait_bytes(ci, rsem.at[CB])

        wait_bytes(kbuf.at[pl.ds(0, 6)], rsem.at[K2])

    def bulk_finish():
        wait_bytes(kbuf.at[pl.ds(0, 4)], ssem.at[K1])
        wait_bytes(kbuf.at[pl.ds(0, 6)], ssem.at[K2])

        @pl.when(serves)
        def _():
            wait_bytes(ci.at[pl.ds(0, 2)], ssem.at[CA])

        @pl.when(direct)
        def _():
            wait_bytes(ci.at[0], ssem.at[CR])

        @pl.when(jnp.logical_not(at_source))
        def _():
            wait_bytes(ci.at[pl.ds(0, 2)], ssem.at[CB])

        @pl.when(is_home)
        def _():
            wait_bytes(ci, ssem.at[CB])

    finish.append(bulk_finish)
    bulk_direct(0)
    for b in range(2):
        kbuf[5 + b] = kc_ref[0, b]

    plus = []
    for j in range(FINE):
        home = c * 2 + j // KR
        flag = map_ref[1, c * FINE + j] == lax.rem(home + 1, ROWS)
        plus.append(flag.astype(F32))

    def split(v):
        high = v.astype(BF16)
        return high, (v - high.astype(F32)).astype(BF16)

    def restrict(parts, app):
        acc = [jnp.zeros((VS, BANDS), F32) for _ in range(4)]
        for j in range(FINE):
            home = 1 + j // KR
            high, low = split(parts[j])
            both = jnp.concatenate([high, low], axis=0)
            up = (both.astype(F32) * plus[j]).astype(BF16)
            down = both - up
            own = mm(both, coef_ref[j, 0], NT)
            side = mm(jnp.concatenate([down, up], axis=0), coef_ref[j, 1], NT)
            acc[home] = acc[home] + own[:VS] + own[VS:]
            acc[home - 1] = acc[home - 1] + side[:VS] + side[VS:2 * VS]
            acc[home + 1] = acc[home + 1] + side[2 * VS:3 * VS] + side[3 * VS:]
        wsend[app] = jnp.concatenate([acc[1], acc[2]], axis=1).astype(BF16)
        wside[app, 0] = acc[0].astype(BF16)
        wside[app, 1] = acc[3].astype(BF16)
        sem = APP + 4 * app
        for t in OFFSETS:
            tr = plane_row(t)
            remote(wside.at[app, 0], whigh.at[app, r], sem, tr, c_prev)
            remote(wside.at[app, 1], wlow.at[app, r], sem + 1, tr, c_next)
            if t == (0, 0):
                local(wsend.at[app], wfull.at[app, r], sem + 2)
            else:
                remote(wsend.at[app], wfull.at[app, r], sem + 2, tr, c)
        finish_plain(sem, whigh.at[app])
        finish_plain(sem + 1, wlow.at[app])
        finish_plain(sem + 2, wfull.at[app, pl.ds(0, ROWS - 1)])

    def coarse_apply(app):
        sem = APP + 4 * app
        wait_bytes(wfull.at[app], rsem.at[sem + 2])
        wait_bytes(whigh.at[app], rsem.at[sem])
        wait_bytes(wlow.at[app], rsem.at[sem + 1])
        full = wfull[app].reshape(NVEC, 2 * BANDS)
        left = full[:, :BANDS].astype(F32) + wlow[app].reshape(NVEC, BANDS).astype(F32)
        right = full[:, BANDS:].astype(F32) + whigh[app].reshape(NVEC, BANDS).astype(F32)
        part = mm(left.astype(BF16), kc_ref[0, 0], NT) + mm(right.astype(BF16), kc_ref[0, 1], NT)
        usend[app] = part.astype(BF16).reshape(ROWS, VS, BANDS)
        for t in OFFSETS:
            tr = plane_row(t)
            src = usend.at[app, tr]
            own = ured.at[app, (1 + odd) * COLS + c]
            near = ured.at[app, 3 * (1 - odd) * COLS + c]
            if t == (0, 0):
                either(is_diag, src, own, sem + 3, tr, diag_col)
                either(is_near, src, near, sem + 3, tr, near_col)
            else:
                remote(src, own, sem + 3, tr, diag_col)
                remote(src, near, sem + 3, tr, near_col)
        finish_but_one(jnp.logical_or(is_diag, is_near), sem + 3, ured.at[app], 4 * COLS)

    def reduce_coarse(app):
        wait_bytes(ured.at[app], rsem.at[APP + 4 * app + 3])
        u = []
        for h in range(4):
            total = ured[app, h * COLS].astype(F32)
            for t in range(1, COLS):
                total = total + ured[app, h * COLS + t].astype(F32)
            u.append(total)
        return u

    def prolong(u, j):
        home = 1 + j // KR
        side = u[home - 1] * (1.0 - plus[j]) + u[home + 1] * plus[j]
        value = mm(jnp.concatenate(split(u[home]), axis=0), coef_ref[j, 0], NN)
        value = value + mm(jnp.concatenate(split(side), axis=0), coef_ref[j, 1], NN)
        return value[:VS] + value[VS:]

    def to_native(src, dst, sem):
        for t in OFFSETS:
            dy, dx = t
            q = lax.rem(odd * COLS + c + 4 * dy + dx, ROWS)
            tr = first_row + lax.div(q, COLS)
            tc = lax.rem(q, COLS)
            if t == (0, 0):
                either(is_diag, src.at[q], dst.at[r], sem, tr, tc)
            else:
                remote(src.at[q], dst.at[r], sem, tr, tc)
        finish_but_one(is_diag, sem, src, ROWS)

    lanes = lax.broadcasted_iota(jnp.int32, (VS, HALF), 1)
    vecs = lax.broadcasted_iota(jnp.int32, (VS, HALF), 0)

    def place(shift):
        return lanes == vecs + VS * shift

    own_place = place(lax.rem(r, 8))

    def as_row(v):
        return jnp.sum(jnp.where(own_place, v, 0.0), axis=0, keepdims=True)

    def as_column(row, mask):
        return jnp.sum(jnp.where(mask, row, 0.0), axis=1, keepdims=True)

    def s_block(j):
        return jnp.concatenate([scol[2 * j], scol[2 * j + 1]], axis=1) * PRESCALE

    def d_block(j):
        return jnp.concatenate([ecol[2 * j], ecol[2 * j + 1]], axis=1) - SHIFT

    def row_sum(v):
        return jnp.sum(v, axis=1, keepdims=True)

    def left_part():
        for i in range(KR):
            for n in range(2):
                cit[i, n] = ci[i, n].T
        for i in range(KR):
            flag = map_ref[1, r * KR + i] == r_next
            row = jnp.where(flag, 8, 0)
            for b in range(4):
                value = mm(cit[i, 0], kbuf[4 + b], NN) + mm(cit[i, 1], kbuf[row + b], NN)
                lbuf[b, pl.ds(i * BANDS, BANDS), :] = value.astype(BF16)

    def tile_piece(j):
        home = 1 + j // KR
        flag = map_ref[1, c * FINE + j] == lax.rem(c * 2 + j // KR + 1, ROWS)
        other = jnp.where(flag, home + 1, home - 1)
        for m in range(KR):
            rows = pl.ds(m * BANDS, BANDS)
            value = mm(lbuf[home, rows], coef_ref[j, 0], NN) + mm(lbuf[other, rows], coef_ref[j, 1], NN)
            tbuf[j, rows, :] = value.astype(BF16)
        pltpu.make_async_copy(
            tbuf.at[j], tile_ref.at[:, pl.ds(j * BANDS, BANDS)], tsem.at[j]
        ).start()

    wait_bytes(scol, rsem.at[S])
    restrict([s_block(j) for j in range(FINE)], 0)
    bulk_direct(1)
    coarse_apply(0)
    bulk_second()
    u = reduce_coarse(0)
    wait_bytes(ecol, rsem.at[E])
    parts = []
    ss = sg = gg = jnp.zeros((VS, 1), F32)
    for j in range(FINE):
        s_j = s_block(j)
        g_j = prolong(u, j) + d_block(j) * s_j
        gcol[j] = g_j
        parts.append(g_j)
        ss = ss + row_sum(s_j * s_j)
        sg = sg + row_sum(s_j * g_j)
        gg = gg + row_sum(g_j * g_j)

    restrict(parts, 1)
    for n, v in enumerate((ss, sg, gg)):
        zs_send[n] = as_row(v)
    local(zs_send, zs_recv.at[c], ZS)
    for t in range(1, COLS):
        remote(zs_send, zs_recv.at[c], ZS, r, lax.rem(c + t, COLS))
    finish_plain(ZS, zs_recv.at[pl.ds(0, COLS - 1)])
    bulk_siblings()
    bulk_wait()
    left_part()
    wait_bytes(zs_recv, rsem.at[ZS])
    mean = zs_recv[0]
    for t in range(1, COLS):
        mean = mean + zs_recv[t]
    mean = mean / ORDER
    ss, sg, gg = (as_column(mean[n], own_place) for n in range(3))
    var = ss + EPS * PRESCALE * PRESCALE
    scale = jnp.sqrt(var)
    alpha_one = (sg + SHIFT * ss) / var
    mix = SHIFT - alpha_one
    remain_sq = (gg + 2.0 * mix * sg + mix * mix * ss) / var
    beta = jnp.sqrt(jnp.maximum(remain_sq, 0.0) + EPS)
    inv = 1.0 / (scale * beta)
    ab_send[0] = as_row(alpha_one)
    ab_send[1] = as_row(beta)
    for j in range(FINE):
        sec = (gcol[j] + mix * s_block(j)) * inv
        for h in range(2):
            sec_send[2 * j + h] = sec[:, h * HALF:(h + 1) * HALF]
    to_native(sec_send, sec_nat, SEC)
    for t in OFFSETS:
        if t == (0, 0):
            local(ab_send, ab_recv.at[r], AB)
        else:
            remote(ab_send, ab_recv.at[r], AB, plane_row(t), c)
    finish_plain(AB, ab_recv.at[pl.ds(0, ROWS - 1)])
    coarse_apply(1)
    for j in range(4):
        tile_piece(j)

    u = reduce_coarse(1)
    over = beta / scale
    dot = jnp.zeros((VS, 1), F32)
    for j in range(FINE):
        s_j = s_block(j)
        g_j = gcol[j]
        h_j = prolong(u, j) + d_block(j) * g_j
        sec = jnp.concatenate([sec_send[2 * j], sec_send[2 * j + 1]], axis=1)
        shifted = (h_j + mix * g_j) * inv + SHIFT * sec - over * s_j
        dot = dot + row_sum(sec * shifted)
        for h in range(2):
            sh_send[2 * j + h] = shifted[:, h * HALF:(h + 1) * HALF]
    dot_send[...] = as_row(dot)
    for tz in AROUND:
        for t in OFFSETS:
            if t == (0, 0) and tz == 0:
                local(dot_send, dot_recv.at[c * ROWS + r], DOT)
            else:
                remote(dot_send, dot_recv.at[c * ROWS + r], DOT, plane_row(t), lax.rem(c + tz, COLS))
    finish_plain(DOT, dot_recv.at[pl.ds(0, ROWS * COLS - 1)])
    to_native(sh_send, sh_nat, SH)
    for j in range(4, FINE):
        tile_piece(j)

    wait_bytes(sec_nat, rsem.at[SEC])
    second_ref[...] = sec_nat[...].reshape(NVEC, HALF)
    wait_bytes(ab_recv, rsem.at[AB])
    wait_bytes(dot_recv, rsem.at[DOT])
    wait_bytes(sh_nat, rsem.at[SH])
    total = dot_recv[pl.ds(0, ROWS)]
    for t in range(1, COLS):
        total = total + dot_recv[pl.ds(t * ROWS, ROWS)]
    alpha_two = total / ORDER

    for i in range(ROWS):
        column = as_column(alpha_two[i], place(i % 8))
        resid_ref[pl.ds(i * VS, VS), :] = sh_nat[i] - column * sec_nat[i]
    rows = []
    for get in (lambda i: ab_recv[i, 0], lambda i: ab_recv[i, 1], lambda i: alpha_two[i]):
        halves = []
        for h in range(2):
            value = get(8 * h)
            for i in range(1, 8):
                value = value + get(8 * h + i)
            halves.append(value)
        rows.append(jnp.concatenate(halves, axis=1))
    coeffs_ref[...] = jnp.concatenate(rows, axis=0)

    for j in range(FINE):
        pltpu.make_async_copy(
            tbuf.at[j], tile_ref.at[:, pl.ds(j * BANDS, BANDS)], tsem.at[j]
        ).wait()
    for run in finish:
        run()


def per_device(coarse_kernel, interp_coef, interp_map, energy, start_vectors):
    vmem = pl.BlockSpec(memory_space=pltpu.VMEM)
    anywhere = pl.BlockSpec(memory_space=pl.ANY)
    nsem = 12 + 8
    return pl.pallas_call(
        kernel,
        out_shape=(
            jax.ShapeDtypeStruct((NVEC, HALF), F32),
            jax.ShapeDtypeStruct((NVEC, HALF), F32),
            jax.ShapeDtypeStruct((3, NVEC), F32),
            jax.ShapeDtypeStruct((KR * BANDS, FINE * BANDS), BF16),
        ),
        in_specs=[pl.BlockSpec(memory_space=pltpu.SMEM), anywhere, anywhere, anywhere, anywhere],
        out_specs=(vmem, vmem, vmem, anywhere),
        scratch_shapes=[
            pltpu.VMEM((1, 2, BANDS, BANDS), BF16),
            pltpu.VMEM((FINE, 2, BANDS, BANDS), BF16),
            pltpu.VMEM((1, HALF), F32),
            pltpu.VMEM((NVEC, HALF), F32),
            pltpu.VMEM((16, VS, HALF), F32),
            pltpu.VMEM((16, 1, HALF), F32),
            pltpu.VMEM((FINE, VS, BANDS), F32),
            pltpu.VMEM((12, BANDS, BANDS), BF16),
            pltpu.VMEM((KR, 2, BANDS, BANDS), BF16),
            pltpu.VMEM((KR, 2, BANDS, BANDS), BF16),
            pltpu.VMEM((4, KR * BANDS, BANDS), BF16),
            pltpu.VMEM((FINE, KR * BANDS, BANDS), BF16),
            pltpu.VMEM((2, VS, 2 * BANDS), BF16),
            pltpu.VMEM((2, 2, VS, BANDS), BF16),
            pltpu.VMEM((2, ROWS, VS, 2 * BANDS), BF16),
            pltpu.VMEM((2, ROWS, VS, BANDS), BF16),
            pltpu.VMEM((2, ROWS, VS, BANDS), BF16),
            pltpu.VMEM((2, ROWS, VS, BANDS), BF16),
            pltpu.VMEM((2, 4 * COLS, VS, BANDS), BF16),
            pltpu.VMEM((3, 1, HALF), F32),
            pltpu.VMEM((COLS, 3, 1, HALF), F32),
            pltpu.VMEM((2, 1, HALF), F32),
            pltpu.VMEM((ROWS, 2, 1, HALF), F32),
            pltpu.VMEM((16, VS, HALF), F32),
            pltpu.VMEM((16, VS, HALF), F32),
            pltpu.VMEM((16, VS, HALF), F32),
            pltpu.VMEM((16, VS, HALF), F32),
            pltpu.VMEM((1, HALF), F32),
            pltpu.VMEM((COLS * ROWS, 1, HALF), F32),
            pltpu.SemaphoreType.DMA((nsem,)),
            pltpu.SemaphoreType.DMA((nsem,)),
            pltpu.SemaphoreType.DMA((FINE,)),
            pltpu.SemaphoreType.DMA((4,)),
        ],
        compiler_params=pltpu.CompilerParams(
            has_side_effects=True, collective_id=0, vmem_limit_bytes=60 * 1024 * 1024
        ),
    )(interp_map.T, coarse_kernel, interp_coef, energy.reshape(1, HALF), start_vectors)


def solution(mesh):
    return jax.shard_map(
        per_device,
        mesh=mesh,
        in_specs=(
            P("row", "col", None, None),
            P("col", None, None, None),
            P(),
            P(("row", "col")),
            P(None, ("row", "col")),
        ),
        out_specs=(P(None, ("row", "col")), P(None, ("row", "col")), P(), P("row", "col")),
        check_vma=False,
    )
```

time: 102 us -> 81.8 us (0.80)
  Pallas kernels: 91.9 us -> 71.7 us
    pallas_call x1, Pallas kernels: 91.9 us -> 71.7 us  [per_device(): pl.pallas_call(kernel, out_shape=(jax.ShapeDtypeStruct((NVEC, HALF), F32)...]
    unnamed x12 -> x4, local copies, waits for them, and re-layouts: 8.19 us -> 9.2 us
where the time goes in v2:
time: 81.8 us; the launch traced here: 81.5 us
  Pallas kernels  71.7 us (88%)
  local copies, waits for them, and re-layouts  9.2 us (11%)
    pallas_call x1, Pallas kernels, per_device(): pl.pallas_call(kernel, out_shape=(jax.ShapeDtypeStruct((NVEC, HALF), F32)...  71.7 us
    unnamed x4, local copies, waits for them, and re-layouts  9.2 us

profile of v2, /device:TPU:1, one launch (start us, length us, event | category | flops | bytes accessed | tf_op | source)
XLA Modules:
  0.0 81.5 jit_solution(17202984487633182536)
XLA Ops:
  0.6 71.7 %shard_map.84 = (f32[256,128]{1,0:T(8,128)}, f32[256,128]{1,0:T(8,128)}, f32[3,256]{1,0:T(4,128)}, bf16[1024,2048]{1,0:T(8,128)(2,1)}) custom-call(s32[2,64]{1,0:T(2,128)} %bitcast.2, bf16[1,2,256,256]{3,2,1,0:T(8,128)(2,1)} %kc_hbm.1, bf16[8,2,256,256]{3,2,1,0:T(8,128)(2,1)} %coef_hbm.1, f32[1,128]{1,0:T(1,128)} %bitcast.3, f32[256,128]{1,0:T(8,128)} %s_hbm.1), custom_call_target="tpu_custom_call" | custom-call | tf_op jit(solution)/shard_map/pallas_call | solution.py:498
  72.3 1.6 %copy.13 = f32[256,128]{1,0:T(8,128)} copy(f32[256,128]{1,0:T(8,128)} %get-tuple-element.8) | data formatting | bytes 262144
  73.9 1.6 %copy.14 = f32[256,128]{1,0:T(8,128)} copy(f32[256,128]{1,0:T(8,128)} %get-tuple-element.9) | data formatting | bytes 262144
  75.5 1.3 %copy.15 = f32[3,256]{1,0:T(4,128)} copy(f32[3,256]{1,0:T(4,128)} %get-tuple-element.10) | data formatting | bytes 6144
  76.8 4.8 %copy.16 = bf16[1024,2048]{1,0:T(8,128)(2,1)} copy(bf16[1024,2048]{1,0:T(8,128)(2,1)} %get-tuple-element.11) | data formatting | bytes 8388608

commit v3 on v2

--- a/solution.py
+++ b/solution.py
@@ -41,13 +41,13 @@
 
 
 def kernel(
-    map_ref, kc_hbm, coef_hbm, e_hbm, s_hbm,
+    map_hbm, kc_hbm, coef_hbm, e_hbm, s_hbm,
     second_ref, resid_ref, coeffs_ref, tile_ref,
-    kc_ref, coef_ref, e_ref, s_ref,
-    scol, ecol, gcol, kbuf, ci, cit, lbuf, tbuf,
+    map_ref, kc_ref, coef_ref, e_ref, s_ref,
+    scol, ecol, gcol, kbuf, cj, ci, cit, lbuf,
     wsend, wside, wfull, wlow, whigh, usend, ured,
-    zs_send, zs_recv, ab_send, ab_recv, sec_send, sec_nat, sh_send, sh_nat, dot_send, dot_recv,
-    ssem, rsem, tsem, lsem,
+    zs_send, zs_recv, ab_send, ab_recv, y_send, y_nat, z_send, z_nat, dot_send, dot_recv,
+    ssem, rsem, lsem,
 ):
     r = lax.axis_index("row")
     c = lax.axis_index("col")
@@ -67,7 +67,7 @@
     finish = []
 
     loads = []
-    for n, (src, dst) in enumerate(((s_hbm, s_ref), (e_hbm, e_ref), (kc_hbm, kc_ref), (coef_hbm, coef_ref))):
+    for n, (src, dst) in enumerate(((s_hbm, s_ref), (e_hbm, e_ref), (kc_hbm, kc_ref), (coef_hbm, coef_ref), (map_hbm, map_ref))):
         loads.append(pltpu.make_async_copy(src, dst, lsem.at[n]))
         loads[-1].start()
 
@@ -86,9 +86,10 @@
                 greet(plane_row(t), lax.rem(c + tz, COLS))
     pl.semaphore_wait(barrier, ROWS * COLS - 1)
 
-    def remote(src, dst, sem, tr, tc):
+    def remote(src, dst, sem, tr, tc, out=None):
         pltpu.make_async_remote_copy(
-            src_ref=src, dst_ref=dst, send_sem=ssem.at[sem], recv_sem=rsem.at[sem],
+            src_ref=src, dst_ref=dst, recv_sem=rsem.at[sem],
+            send_sem=ssem.at[sem if out is None else out],
             device_id=(tr, tc), device_id_type=MESH,
         ).start()
 
@@ -119,7 +120,8 @@
 
         finish.append(run)
 
-    S, E, K1, K2, CA, CR, CB, AB, SEC, SH, DOT, ZS, APP = range(13)
+    S, E, K1, K2, CB, AB, YN, ZN, DOT, ZS = range(10)
+    C1, C3, APP = 10, 14, 18
 
     loads[0].wait()
     loads[1].wait()
@@ -142,68 +144,75 @@
     finish_but_one(is_diag, E, ecol, ROWS)
     loads[2].wait()
     loads[3].wait()
-
-    serves = lax.div(x, 2) == k
+    loads[4].wait()
+
     delta = lax.rem(y - z + 4, 4)
     mine = lax.rem(x, 2) * KR + delta
-    away = lax.rem(z - y + 4, 4)
-    at_source = away == 0
     home_core = lax.div(x, 2)
-    is_home = jnp.logical_and(at_source, k == home_core)
-    direct = jnp.logical_or(away == 1, away == 3)
+    at_source = delta == 0
+    serves = k == home_core
+    is_home = jnp.logical_and(at_source, serves)
     r_next = lax.rem(r + 1, ROWS)
     r_prev = lax.rem(r + ROWS - 1, ROWS)
     pair = pl.ds(2 * k, 2)
-
-    def bulk_direct(b):
-        remote(kc_ref.at[0, b], kbuf.at[1 + b], K1, r_next, c)
-        remote(kc_ref.at[0, b], kbuf.at[9 + b], K1, r_prev, c)
+    piece = [lax.rem(delta + t, 4) for t in range(4)]
+    holds = [lax.div(p, 2) == k for p in piece]
+
+    def ring_col(t, core):
+        return 2 * lax.rem(z + t, 4) + core
+
+    def bulk_first():
+        remote(kc_ref.at[0], kbuf.at[pl.ds(1, 2)], K1, r_next, c)
+        remote(kc_ref.at[0], kbuf.at[pl.ds(9, 2)], K1, r_prev, c)
 
         @pl.when(serves)
         def _():
             for t in (1, 3):
-                remote(
-                    coef_ref.at[mine, b], ci.at[delta, b], CA,
-                    4 * z + x, 2 * lax.rem(z + t, 4) + lax.div(delta, 2),
-                )
+                remote(coef_ref.at[mine], cj.at[t], C1 + t, r, ring_col(t, lax.div(delta, 2)), C1)
 
     def bulk_second():
+        for t in (1, 3):
+            @pl.when(holds[t])
+            def _(t=t):
+                wait_bytes(cj.at[t], rsem.at[C1 + t])
+                n = t // 2
+                remote(cj.at[t, n], cj.at[2, n], C1 + 2, r, ring_col(t, k), C1 + t)
+
         wait_bytes(kbuf.at[pl.ds(0, 4)], rsem.at[K1])
         for slot in range(3):
             remote(kbuf.at[4 * slot + 1], kbuf.at[4 * slot + 3], K2, r, c_prev)
             remote(kbuf.at[4 * slot + 2], kbuf.at[4 * slot], K2, r, c_next)
 
-        @pl.when(direct)
-        def _():
-            wait_bytes(ci.at[pl.ds(0, 2)], rsem.at[CA])
-
-        @pl.when(away == 1)
-        def _():
-            remote(ci.at[pair, 0], ci.at[pair, 0], CR, r, 2 * lax.rem(z + 1, 4) + k)
-
-        @pl.when(away == 3)
-        def _():
-            remote(ci.at[pair, 1], ci.at[pair, 1], CR, r, 2 * lax.rem(z + 3, 4) + k)
+    def bulk_third():
+        @pl.when(holds[2])
+        def _():
+            wait_bytes(cj.at[2], rsem.at[C1 + 2])
+
+        for t in (1, 2, 3):
+            @pl.when(jnp.logical_and(holds[t], piece[t] != 0))
+            def _(t=t):
+                remote(cj.at[t], ci.at[piece[t]], C3, 4 * lax.rem(z + 4 - t, 4) + x, c, C3 + t)
+
+            @pl.when(jnp.logical_and(holds[t], piece[t] == 0))
+            def _(t=t):
+                local(cj.at[t], ci.at[0], C3)
 
     def bulk_siblings():
-        @pl.when(away == 2)
-        def _():
-            wait_bytes(ci.at[pl.ds(0, 2)], rsem.at[CR])
-
         @pl.when(jnp.logical_not(at_source))
         def _():
+            wait_bytes(ci.at[pl.ds(0, 2)], rsem.at[C3])
             remote(ci.at[pair], ci.at[pair], CB, r, sibling)
 
         @pl.when(is_home)
         def _():
             src = coef_ref.at[pl.ds(odd * KR, KR)]
-            local(src, ci, CA)
+            local(src, ci, C1)
             remote(src, ci, CB, r, sibling)
 
     def bulk_wait():
         @pl.when(is_home)
         def _():
-            wait_bytes(ci, rsem.at[CA])
+            wait_bytes(ci, rsem.at[C1])
 
         @pl.when(jnp.logical_not(at_source))
         def _():
@@ -221,11 +230,17 @@
 
         @pl.when(serves)
         def _():
-            wait_bytes(ci.at[pl.ds(0, 2)], ssem.at[CA])
-
-        @pl.when(direct)
-        def _():
-            wait_bytes(ci.at[0], ssem.at[CR])
+            wait_bytes(ci.at[pl.ds(0, 2)], ssem.at[C1])
+
+        for t in (1, 3):
+            @pl.when(holds[t])
+            def _(t=t):
+                wait_bytes(kbuf.at[0], ssem.at[C1 + t])
+
+        for t in (1, 2, 3):
+            @pl.when(jnp.logical_and(holds[t], piece[t] != 0))
+            def _(t=t):
+                wait_bytes(ci.at[0], ssem.at[C3 + t])
 
         @pl.when(jnp.logical_not(at_source))
         def _():
@@ -236,7 +251,7 @@
             wait_bytes(ci, ssem.at[CB])
 
     finish.append(bulk_finish)
-    bulk_direct(0)
+    bulk_first()
     for b in range(2):
         kbuf[5 + b] = kc_ref[0, b]
 
@@ -285,9 +300,9 @@
         wait_bytes(whigh.at[app], rsem.at[sem])
         wait_bytes(wlow.at[app], rsem.at[sem + 1])
         full = wfull[app].reshape(NVEC, 2 * BANDS)
-        left = full[:, :BANDS].astype(F32) + wlow[app].reshape(NVEC, BANDS).astype(F32)
-        right = full[:, BANDS:].astype(F32) + whigh[app].reshape(NVEC, BANDS).astype(F32)
-        part = mm(left.astype(BF16), kc_ref[0, 0], NT) + mm(right.astype(BF16), kc_ref[0, 1], NT)
+        part = mm(full[:, :BANDS], kc_ref[0, 0], NT) + mm(full[:, BANDS:], kc_ref[0, 1], NT)
+        part = part + mm(wlow[app].reshape(NVEC, BANDS), kc_ref[0, 0], NT)
+        part = part + mm(whigh[app].reshape(NVEC, BANDS), kc_ref[0, 1], NT)
         usend[app] = part.astype(BF16).reshape(ROWS, VS, BANDS)
         for t in OFFSETS:
             tr = plane_row(t)
@@ -351,6 +366,10 @@
     def d_block(j):
         return jnp.concatenate([ecol[2 * j], ecol[2 * j + 1]], axis=1) - SHIFT
 
+    def keep(buf, j, v):
+        for h in range(2):
+            buf[2 * j + h] = v[:, h * HALF:(h + 1) * HALF].astype(BF16)
+
     def row_sum(v):
         return jnp.sum(v, axis=1, keepdims=True)
 
@@ -372,25 +391,24 @@
         for m in range(KR):
             rows = pl.ds(m * BANDS, BANDS)
             value = mm(lbuf[home, rows], coef_ref[j, 0], NN) + mm(lbuf[other, rows], coef_ref[j, 1], NN)
-            tbuf[j, rows, :] = value.astype(BF16)
-        pltpu.make_async_copy(
-            tbuf.at[j], tile_ref.at[:, pl.ds(j * BANDS, BANDS)], tsem.at[j]
-        ).start()
+            tile_ref[rows, pl.ds(j * BANDS, BANDS)] = value.astype(BF16)
 
     wait_bytes(scol, rsem.at[S])
     restrict([s_block(j) for j in range(FINE)], 0)
-    bulk_direct(1)
+    bulk_second()
     coarse_apply(0)
-    bulk_second()
+    bulk_third()
     u = reduce_coarse(0)
     wait_bytes(ecol, rsem.at[E])
     parts = []
     ss = sg = gg = jnp.zeros((VS, 1), F32)
     for j in range(FINE):
         s_j = s_block(j)
-        g_j = prolong(u, j) + d_block(j) * s_j
+        y_j = prolong(u, j)
+        g_j = y_j + d_block(j) * s_j
         gcol[j] = g_j
         parts.append(g_j)
+        keep(y_send, j, y_j)
         ss = ss + row_sum(s_j * s_j)
         sg = sg + row_sum(s_j * g_j)
         gg = gg + row_sum(g_j * g_j)
@@ -402,9 +420,6 @@
     for t in range(1, COLS):
         remote(zs_send, zs_recv.at[c], ZS, r, lax.rem(c + t, COLS))
     finish_plain(ZS, zs_recv.at[pl.ds(0, COLS - 1)])
-    bulk_siblings()
-    bulk_wait()
-    left_part()
     wait_bytes(zs_recv, rsem.at[ZS])
     mean = zs_recv[0]
     for t in range(1, COLS):
@@ -418,35 +433,32 @@
     remain_sq = (gg + 2.0 * mix * sg + mix * mix * ss) / var
     beta = jnp.sqrt(jnp.maximum(remain_sq, 0.0) + EPS)
     inv = 1.0 / (scale * beta)
-    ab_send[0] = as_row(alpha_one)
-    ab_send[1] = as_row(beta)
-    for j in range(FINE):
-        sec = (gcol[j] + mix * s_block(j)) * inv
-        for h in range(2):
-            sec_send[2 * j + h] = sec[:, h * HALF:(h + 1) * HALF]
-    to_native(sec_send, sec_nat, SEC)
+    over = beta / scale
+    for n, v in enumerate((alpha_one, beta, inv, over)):
+        ab_send[n] = as_row(v)
+    coarse_apply(1)
     for t in OFFSETS:
         if t == (0, 0):
             local(ab_send, ab_recv.at[r], AB)
         else:
             remote(ab_send, ab_recv.at[r], AB, plane_row(t), c)
     finish_plain(AB, ab_recv.at[pl.ds(0, ROWS - 1)])
-    coarse_apply(1)
-    for j in range(4):
-        tile_piece(j)
+    to_native(y_send, y_nat, YN)
+    bulk_siblings()
+    bulk_wait()
+    left_part()
 
     u = reduce_coarse(1)
-    over = beta / scale
     dot = jnp.zeros((VS, 1), F32)
     for j in range(FINE):
         s_j = s_block(j)
         g_j = gcol[j]
-        h_j = prolong(u, j) + d_block(j) * g_j
-        sec = jnp.concatenate([sec_send[2 * j], sec_send[2 * j + 1]], axis=1)
+        z_j = prolong(u, j)
+        h_j = z_j + d_block(j) * g_j
+        sec = (g_j + mix * s_j) * inv
         shifted = (h_j + mix * g_j) * inv + SHIFT * sec - over * s_j
         dot = dot + row_sum(sec * shifted)
-        for h in range(2):
-            sh_send[2 * j + h] = shifted[:, h * HALF:(h + 1) * HALF]
+        keep(z_send, j, z_j)
     dot_send[...] = as_row(dot)
     for tz in AROUND:
         for t in OFFSETS:
@@ -455,24 +467,30 @@
             else:
                 remote(dot_send, dot_recv.at[c * ROWS + r], DOT, plane_row(t), lax.rem(c + tz, COLS))
     finish_plain(DOT, dot_recv.at[pl.ds(0, ROWS * COLS - 1)])
-    to_native(sh_send, sh_nat, SH)
-    for j in range(4, FINE):
+    to_native(z_send, z_nat, ZN)
+    for j in range(FINE):
         tile_piece(j)
 
-    wait_bytes(sec_nat, rsem.at[SEC])
-    second_ref[...] = sec_nat[...].reshape(NVEC, HALF)
+    wait_bytes(y_nat, rsem.at[YN])
     wait_bytes(ab_recv, rsem.at[AB])
+    diag = e_ref[...] - SHIFT
+    for i in range(ROWS):
+        rows = pl.ds(i * VS, VS)
+        mask = place(i % 8)
+        first = s_ref[rows, :] * PRESCALE
+        image = y_nat[i].astype(F32) + diag * first
+        mix_i = SHIFT - as_column(ab_recv[i, 0], mask)
+        inv_i = as_column(ab_recv[i, 2], mask)
+        over_i = as_column(ab_recv[i, 3], mask)
+        sec = (image + mix_i * first) * inv_i
+        second_ref[rows, :] = sec
+        resid_ref[rows, :] = (diag * image + mix_i * image) * inv_i + SHIFT * sec - over_i * first
     wait_bytes(dot_recv, rsem.at[DOT])
-    wait_bytes(sh_nat, rsem.at[SH])
     total = dot_recv[pl.ds(0, ROWS)]
     for t in range(1, COLS):
         total = total + dot_recv[pl.ds(t * ROWS, ROWS)]
     alpha_two = total / ORDER
-
-    for i in range(ROWS):
-        column = as_column(alpha_two[i], place(i % 8))
-        resid_ref[pl.ds(i * VS, VS), :] = sh_nat[i] - column * sec_nat[i]
-    rows = []
+    lines = []
     for get in (lambda i: ab_recv[i, 0], lambda i: ab_recv[i, 1], lambda i: alpha_two[i]):
         halves = []
         for h in range(2):
@@ -480,32 +498,46 @@
             for i in range(1, 8):
                 value = value + get(8 * h + i)
             halves.append(value)
-        rows.append(jnp.concatenate(halves, axis=1))
-    coeffs_ref[...] = jnp.concatenate(rows, axis=0)
-
-    for j in range(FINE):
-        pltpu.make_async_copy(
-            tbuf.at[j], tile_ref.at[:, pl.ds(j * BANDS, BANDS)], tsem.at[j]
-        ).wait()
+        lines.append(jnp.concatenate(halves, axis=1))
+    coeffs_ref[...] = jnp.concatenate(lines, axis=0)
+    wait_bytes(z_nat, rsem.at[ZN])
+    for i in range(ROWS):
+        rows = pl.ds(i * VS, VS)
+        mask = place(i % 8)
+        column = as_column(alpha_two[i], mask)
+        inv_i = as_column(ab_recv[i, 2], mask)
+        resid_ref[rows, :] = resid_ref[rows, :] + z_nat[i].astype(F32) * inv_i - column * second_ref[rows, :]
+
     for run in finish:
         run()
 
 
+def write_out(*refs):
+    copies = [pltpu.make_async_copy(refs[n], refs[4 + n], refs[8].at[n]) for n in range(4)]
+    for copy in copies:
+        copy.start()
+    for copy in copies:
+        copy.wait()
+
+
 def per_device(coarse_kernel, interp_coef, interp_map, energy, start_vectors):
     vmem = pl.BlockSpec(memory_space=pltpu.VMEM)
-    anywhere = pl.BlockSpec(memory_space=pl.ANY)
-    nsem = 12 + 8
-    return pl.pallas_call(
+    hbm = pl.BlockSpec(memory_space=pltpu.HBM)
+    nsem = 18 + 8
+    shapes = (
+        jax.ShapeDtypeStruct((NVEC, HALF), F32),
+        jax.ShapeDtypeStruct((NVEC, HALF), F32),
+        jax.ShapeDtypeStruct((3, NVEC), F32),
+        jax.ShapeDtypeStruct((KR * BANDS, FINE * BANDS), BF16),
+    )
+    operands = (interp_map.T, coarse_kernel, interp_coef, energy.reshape(1, HALF), start_vectors)
+    results = pl.pallas_call(
         kernel,
-        out_shape=(
-            jax.ShapeDtypeStruct((NVEC, HALF), F32),
-            jax.ShapeDtypeStruct((NVEC, HALF), F32),
-            jax.ShapeDtypeStruct((3, NVEC), F32),
-            jax.ShapeDtypeStruct((KR * BANDS, FINE * BANDS), BF16),
-        ),
-        in_specs=[pl.BlockSpec(memory_space=pltpu.SMEM), anywhere, anywhere, anywhere, anywhere],
-        out_specs=(vmem, vmem, vmem, anywhere),
+        out_shape=shapes,
+        in_specs=[hbm] * 5,
+        out_specs=(vmem, vmem, vmem, vmem),
         scratch_shapes=[
+            pltpu.SMEM((2, COLS * FINE), jnp.int32),
             pltpu.VMEM((1, 2, BANDS, BANDS), BF16),
             pltpu.VMEM((FINE, 2, BANDS, BANDS), BF16),
             pltpu.VMEM((1, HALF), F32),
@@ -514,10 +546,10 @@
             pltpu.VMEM((16, 1, HALF), F32),
             pltpu.VMEM((FINE, VS, BANDS), F32),
             pltpu.VMEM((12, BANDS, BANDS), BF16),
+            pltpu.VMEM((4, 2, BANDS, BANDS), BF16),
             pltpu.VMEM((KR, 2, BANDS, BANDS), BF16),
             pltpu.VMEM((KR, 2, BANDS, BANDS), BF16),
             pltpu.VMEM((4, KR * BANDS, BANDS), BF16),
-            pltpu.VMEM((FINE, KR * BANDS, BANDS), BF16),
             pltpu.VMEM((2, VS, 2 * BANDS), BF16),
             pltpu.VMEM((2, 2, VS, BANDS), BF16),
             pltpu.VMEM((2, ROWS, VS, 2 * BANDS), BF16),
@@ -527,23 +559,30 @@
             pltpu.VMEM((2, 4 * COLS, VS, BANDS), BF16),
             pltpu.VMEM((3, 1, HALF), F32),
             pltpu.VMEM((COLS, 3, 1, HALF), F32),
-            pltpu.VMEM((2, 1, HALF), F32),
-            pltpu.VMEM((ROWS, 2, 1, HALF), F32),
-            pltpu.VMEM((16, VS, HALF), F32),
-            pltpu.VMEM((16, VS, HALF), F32),
-            pltpu.VMEM((16, VS, HALF), F32),
-            pltpu.VMEM((16, VS, HALF), F32),
+            pltpu.VMEM((4, 1, HALF), F32),
+            pltpu.VMEM((ROWS, 4, 1, HALF), F32),
+            pltpu.VMEM((16, VS, HALF), BF16),
+            pltpu.VMEM((16, VS, HALF), BF16),
+            pltpu.VMEM((16, VS, HALF), BF16),
+            pltpu.VMEM((16, VS, HALF), BF16),
             pltpu.VMEM((1, HALF), F32),
             pltpu.VMEM((COLS * ROWS, 1, HALF), F32),
             pltpu.SemaphoreType.DMA((nsem,)),
             pltpu.SemaphoreType.DMA((nsem,)),
-            pltpu.SemaphoreType.DMA((FINE,)),
-            pltpu.SemaphoreType.DMA((4,)),
+            pltpu.SemaphoreType.DMA((5,)),
         ],
         compiler_params=pltpu.CompilerParams(
-            has_side_effects=True, collective_id=0, vmem_limit_bytes=60 * 1024 * 1024
+            has_side_effects=True, collective_id=0, vmem_limit_bytes=40 * 1024 * 1024
         ),
-    )(interp_map.T, coarse_kernel, interp_coef, energy.reshape(1, HALF), start_vectors)
+    )(*(pltpu.with_memory_space_constraint(v, pltpu.HBM) for v in operands))
+    return pl.pallas_call(
+        write_out,
+        out_shape=shapes,
+        in_specs=[vmem] * 4,
+        out_specs=(hbm,) * 4,
+        scratch_shapes=[pltpu.SemaphoreType.DMA((4,))],
+        compiler_params=pltpu.CompilerParams(vmem_limit_bytes=1024 * 1024),
+    )(*results)
 
 
 def solution(mesh):

time: 81.8 us -> 63.2 us (0.77)
  Pallas kernels: 71.7 us -> 62.5 us
  local copies, waits for them, and re-layouts: 9.2 us -> 0 us
    pallas_call x1 -> x2, Pallas kernels: 71.7 us -> 62.5 us  [the longest x1 60.3 us: per_device(): pl.pallas_call(kernel, out_shape=shapes, in_specs=[hbm] * 5, out_specs=(v...]
    unnamed x4 -> x0, local copies, waits for them, and re-layouts: 9.2 us -> none
where the time goes in v3:
time: 63.2 us; the launch traced here: 63.1 us
  Pallas kernels  62.5 us (99%)
  between operations  0.64 us (1%)
    pallas_call x1, Pallas kernels, per_device(): pl.pallas_call(kernel, out_shape=shapes, in_specs=[hbm] * 5, out_specs=(v...  60.3 us
    pallas_call x1, Pallas kernels, per_device(): pl.pallas_call(write_out, out_shape=shapes, in_specs=[vmem] * 4, out_spec...  2.14 us

profile of v3, /device:TPU:1, one launch (start us, length us, event | category | flops | bytes accessed | tf_op | source)
XLA Modules:
  0.0 63.1 jit_solution(1366494043879898747)
XLA Ops:
  0.6 60.3 %shard_map.84 = (f32[256,128]{1,0:T(8,128)S(1)}, f32[256,128]{1,0:T(8,128)S(1)}, f32[3,256]{1,0:T(4,128)S(1)}, bf16[1024,2048]{1,0:T(8,128)(2,1)S(1)}) custom-call(s32[2,64]{1,0:T(2,128)} %bitcast.2, bf16[1,2,256,256]{3,2,1,0:T(8,128)(2,1)} %kc_hbm.1, bf16[8,2,256,256]{3,2,1,0:T(8,128)(2,1)} %coef_hbm.1, f32[1,128]{1,0:T(1,128)} %bitcast.3, f32[256,128]{1,0:T(8,128)} %s_hbm.1), custom_call_target="tpu_custom_call" | custom-call | tf_op jit(solution)/shard_map/pallas_call | solution.py:534
  61.0 2.1 %shard_map.85 = (f32[256,128]{1,0:T(8,128)}, f32[256,128]{1,0:T(8,128)}, f32[3,256]{1,0:T(4,128)}, bf16[1024,2048]{1,0:T(8,128)(2,1)}) custom-call(f32[256,128]{1,0:T(8,128)S(1)} %get-tuple-element.8.refs_0_, f32[256,128]{1,0:T(8,128)S(1)} %get-tuple-element.9.refs_1_, f32[3,256]{1,0:T(4,128)S(1)} %get-tuple-element.10.refs_2_, ...), custom_call_target="tpu_custom_call" | custom-call | tf_op jit(solution)/shard_map/pallas_call | solution.py:578

commit v4 on v3

--- a/solution.py
+++ b/solution.py
@@ -63,6 +63,8 @@
     is_diag = c == diag_col
     is_near = c == near_col
     first_row = 2 * c
+    r_next = lax.rem(r + 1, ROWS)
+    r_prev = lax.rem(r + ROWS - 1, ROWS)
     sibling = 2 * z + (1 - k)
     finish = []
 
@@ -80,11 +82,21 @@
         dy, dx = t
         return 4 * lax.rem(y + dy, 4) + lax.rem(x + dx, 4)
 
-    for tz in AROUND:
-        for t in OFFSETS:
-            if tz or t != (0, 0):
-                greet(plane_row(t), lax.rem(c + tz, COLS))
-    pl.semaphore_wait(barrier, ROWS * COLS - 1)
+    for q in range(ROWS):
+        tr, tc = first_row + q // COLS, q % COLS
+
+        @pl.when(jnp.logical_not(jnp.logical_and(tr == r, tc == c)))
+        def _(tr=tr, tc=tc):
+            greet(tr, tc)
+
+    for t in OFFSETS:
+        greet(plane_row(t), c_prev)
+        greet(plane_row(t), c_next)
+    for t in range(2, COLS - 1):
+        greet(r, lax.rem(c + t, COLS))
+    greet(r_next, c)
+    greet(r_prev, c)
+    pl.semaphore_wait(barrier, 16 + 32 + 5 + 2 - is_diag.astype(jnp.int32))
 
     def remote(src, dst, sem, tr, tc, out=None):
         pltpu.make_async_remote_copy(
@@ -120,8 +132,8 @@
 
         finish.append(run)
 
-    S, E, K1, K2, CB, AB, YN, ZN, DOT, ZS = range(10)
-    C1, C3, APP = 10, 14, 18
+    S, E, K2, CB, AB, YN, ZN, DOT, ZS = range(9)
+    K1, C1, C3, APP = 9, 11, 15, 19
 
     loads[0].wait()
     loads[1].wait()
@@ -152,8 +164,6 @@
     at_source = delta == 0
     serves = k == home_core
     is_home = jnp.logical_and(at_source, serves)
-    r_next = lax.rem(r + 1, ROWS)
-    r_prev = lax.rem(r + ROWS - 1, ROWS)
     pair = pl.ds(2 * k, 2)
     piece = [lax.rem(delta + t, 4) for t in range(4)]
     holds = [lax.div(p, 2) == k for p in piece]
@@ -161,9 +171,20 @@
     def ring_col(t, core):
         return 2 * lax.rem(z + t, 4) + core
 
+    def row_blocks(b):
+        remote(kc_ref.at[0, b], kbuf.at[1 + b], K1 + b, r_next, c)
+        remote(kc_ref.at[0, b], kbuf.at[9 + b], K1 + b, r_prev, c)
+
+    def column_blocks(b):
+        wait_bytes(kbuf.at[pl.ds(0, 2)], rsem.at[K1 + b])
+        for slot in range(3):
+            if b == 0:
+                remote(kbuf.at[4 * slot + 1], kbuf.at[4 * slot + 3], K2, r, c_prev)
+            else:
+                remote(kbuf.at[4 * slot + 2], kbuf.at[4 * slot], K2, r, c_next)
+
     def bulk_first():
-        remote(kc_ref.at[0], kbuf.at[pl.ds(1, 2)], K1, r_next, c)
-        remote(kc_ref.at[0], kbuf.at[pl.ds(9, 2)], K1, r_prev, c)
+        row_blocks(0)
 
         @pl.when(serves)
         def _():
@@ -178,18 +199,17 @@
                 n = t // 2
                 remote(cj.at[t, n], cj.at[2, n], C1 + 2, r, ring_col(t, k), C1 + t)
 
-        wait_bytes(kbuf.at[pl.ds(0, 4)], rsem.at[K1])
-        for slot in range(3):
-            remote(kbuf.at[4 * slot + 1], kbuf.at[4 * slot + 3], K2, r, c_prev)
-            remote(kbuf.at[4 * slot + 2], kbuf.at[4 * slot], K2, r, c_next)
+        column_blocks(0)
 
     def bulk_third():
+        row_blocks(1)
+
         @pl.when(holds[2])
         def _():
             wait_bytes(cj.at[2], rsem.at[C1 + 2])
 
         for t in (1, 2, 3):
-            @pl.when(jnp.logical_and(holds[t], piece[t] != 0))
+            @pl.when(jnp.logical_and(holds[t], lax.rem(piece[t], 2) == 1))
             def _(t=t):
                 remote(cj.at[t], ci.at[piece[t]], C3, 4 * lax.rem(z + 4 - t, 4) + x, c, C3 + t)
 
@@ -197,6 +217,14 @@
             def _(t=t):
                 local(cj.at[t], ci.at[0], C3)
 
+        far_piece(0)
+
+    def far_piece(n):
+        for t in (1, 2, 3):
+            @pl.when(jnp.logical_and(holds[t], piece[t] == 2))
+            def _(t=t):
+                remote(cj.at[t, n], ci.at[2, n], C3, 4 * lax.rem(z + 4 - t, 4) + x, c, C3 + t)
+
     def bulk_siblings():
         @pl.when(jnp.logical_not(at_source))
         def _():
@@ -225,7 +253,8 @@
         wait_bytes(kbuf.at[pl.ds(0, 6)], rsem.at[K2])
 
     def bulk_finish():
-        wait_bytes(kbuf.at[pl.ds(0, 4)], ssem.at[K1])
+        wait_bytes(kbuf.at[pl.ds(0, 2)], ssem.at[K1])
+        wait_bytes(kbuf.at[pl.ds(0, 2)], ssem.at[K1 + 1])
         wait_bytes(kbuf.at[pl.ds(0, 6)], ssem.at[K2])
 
         @pl.when(serves)
@@ -266,18 +295,25 @@
         return high, (v - high.astype(F32)).astype(BF16)
 
     def restrict(parts, app):
-        acc = [jnp.zeros((VS, BANDS), F32) for _ in range(4)]
+        acc = [None] * 4
+
+        def add(h, v):
+            acc[h] = v if acc[h] is None else acc[h] + v
+
         for j in range(FINE):
             home = 1 + j // KR
-            high, low = split(parts[j])
-            both = jnp.concatenate([high, low], axis=0)
-            up = (both.astype(F32) * plus[j]).astype(BF16)
-            down = both - up
-            own = mm(both, coef_ref[j, 0], NT)
-            side = mm(jnp.concatenate([down, up], axis=0), coef_ref[j, 1], NT)
-            acc[home] = acc[home] + own[:VS] + own[VS:]
-            acc[home - 1] = acc[home - 1] + side[:VS] + side[VS:2 * VS]
-            acc[home + 1] = acc[home + 1] + side[2 * VS:3 * VS] + side[3 * VS:]
+            both = jnp.concatenate(split(parts[j]), axis=0)
+            add(home, mm(both, coef_ref[j, 0], NT))
+            if j % KR == 0:
+                add(home - 1, mm(both, coef_ref[j, 1], NT))
+            elif j % KR == KR - 1:
+                add(home + 1, mm(both, coef_ref[j, 1], NT))
+            else:
+                up = both * plus[j].astype(BF16)
+                side = mm(jnp.concatenate([both - up, up], axis=0), coef_ref[j, 1], NT)
+                add(home - 1, side[:2 * VS])
+                add(home + 1, side[2 * VS:])
+        acc = [v[:VS] + v[VS:] for v in acc]
         wsend[app] = jnp.concatenate([acc[1], acc[2]], axis=1).astype(BF16)
         wside[app, 0] = acc[0].astype(BF16)
         wside[app, 1] = acc[3].astype(BF16)
@@ -324,14 +360,19 @@
             total = ured[app, h * COLS].astype(F32)
             for t in range(1, COLS):
                 total = total + ured[app, h * COLS + t].astype(F32)
-            u.append(total)
+            u.append(jnp.concatenate(split(total), axis=0))
         return u
 
     def prolong(u, j):
         home = 1 + j // KR
-        side = u[home - 1] * (1.0 - plus[j]) + u[home + 1] * plus[j]
-        value = mm(jnp.concatenate(split(u[home]), axis=0), coef_ref[j, 0], NN)
-        value = value + mm(jnp.concatenate(split(side), axis=0), coef_ref[j, 1], NN)
+        if j % KR == 0:
+            side = u[home - 1]
+        elif j % KR == KR - 1:
+            side = u[home + 1]
+        else:
+            up, down = plus[j].astype(BF16), (1.0 - plus[j]).astype(BF16)
+            side = u[home - 1] * down + u[home + 1] * up
+        value = mm(u[home], coef_ref[j, 0], NN) + mm(side, coef_ref[j, 1], NN)
         return value[:VS] + value[VS:]
 
     def to_native(src, dst, sem):
@@ -420,6 +461,8 @@
     for t in range(1, COLS):
         remote(zs_send, zs_recv.at[c], ZS, r, lax.rem(c + t, COLS))
     finish_plain(ZS, zs_recv.at[pl.ds(0, COLS - 1)])
+    column_blocks(1)
+    far_piece(1)
     wait_bytes(zs_recv, rsem.at[ZS])
     mean = zs_recv[0]
     for t in range(1, COLS):
@@ -445,9 +488,6 @@
     finish_plain(AB, ab_recv.at[pl.ds(0, ROWS - 1)])
     to_native(y_send, y_nat, YN)
     bulk_siblings()
-    bulk_wait()
-    left_part()
-
     u = reduce_coarse(1)
     dot = jnp.zeros((VS, 1), F32)
     for j in range(FINE):
@@ -468,6 +508,8 @@
                 remote(dot_send, dot_recv.at[c * ROWS + r], DOT, plane_row(t), lax.rem(c + tz, COLS))
     finish_plain(DOT, dot_recv.at[pl.ds(0, ROWS * COLS - 1)])
     to_native(z_send, z_nat, ZN)
+    bulk_wait()
+    left_part()
     for j in range(FINE):
         tile_piece(j)
 
@@ -513,7 +555,11 @@
 
 
 def write_out(*refs):
-    copies = [pltpu.make_async_copy(refs[n], refs[4 + n], refs[8].at[n]) for n in range(4)]
+    sems = refs[8]
+    copies = [pltpu.make_async_copy(refs[n], refs[4 + n], sems.at[n]) for n in range(3)]
+    for n in range(8):
+        rows = pl.ds(n * 128, 128)
+        copies.append(pltpu.make_async_copy(refs[3].at[rows], refs[7].at[rows], sems.at[3 + n]))
     for copy in copies:
         copy.start()
     for copy in copies:
@@ -523,7 +569,7 @@
 def per_device(coarse_kernel, interp_coef, interp_map, energy, start_vectors):
     vmem = pl.BlockSpec(memory_space=pltpu.VMEM)
     hbm = pl.BlockSpec(memory_space=pltpu.HBM)
-    nsem = 18 + 8
+    nsem = 19 + 8
     shapes = (
         jax.ShapeDtypeStruct((NVEC, HALF), F32),
         jax.ShapeDtypeStruct((NVEC, HALF), F32),
@@ -580,7 +626,7 @@
         out_shape=shapes,
         in_specs=[vmem] * 4,
         out_specs=(hbm,) * 4,
-        scratch_shapes=[pltpu.SemaphoreType.DMA((4,))],
+        scratch_shapes=[pltpu.SemaphoreType.DMA((11,))],
         compiler_params=pltpu.CompilerParams(vmem_limit_bytes=1024 * 1024),
     )(*results)
 

time: 63.2 us -> 61.9 us (0.979)
  Pallas kernels: 62.5 us -> 61.2 us
    pallas_call x1, Pallas kernels: 60.3 us -> 59 us  [per_device(): pl.pallas_call(kernel, out_shape=shapes, in_specs=[hbm] * 5, out_specs=(v...]
where the time goes in v4:
time: 61.9 us; the launch traced here: 61.8 us
  Pallas kernels  61.2 us (99%)
  between operations  0.64 us (1%)
    pallas_call x1, Pallas kernels, per_device(): pl.pallas_call(kernel, out_shape=shapes, in_specs=[hbm] * 5, out_specs=(v...  59 us
    pallas_call x1, Pallas kernels, per_device(): pl.pallas_call(write_out, out_shape=shapes, in_specs=[vmem] * 4, out_spec...  2.19 us

profile of v4, /device:TPU:1, one launch (start us, length us, event | category | flops | bytes accessed | tf_op | source)
XLA Modules:
  0.0 61.8 jit_solution(10981065127877596967)
XLA Ops:
  0.6 59.0 %shard_map.84 = (f32[256,128]{1,0:T(8,128)S(1)}, f32[256,128]{1,0:T(8,128)S(1)}, f32[3,256]{1,0:T(4,128)S(1)}, bf16[1024,2048]{1,0:T(8,128)(2,1)S(1)}) custom-call(s32[2,64]{1,0:T(2,128)} %bitcast.2, bf16[1,2,256,256]{3,2,1,0:T(8,128)(2,1)} %kc_hbm.1, bf16[8,2,256,256]{3,2,1,0:T(8,128)(2,1)} %coef_hbm.1, f32[1,128]{1,0:T(1,128)} %bitcast.3, f32[256,128]{1,0:T(8,128)} %s_hbm.1), custom_call_target="tpu_custom_call" | custom-call | tf_op jit(solution)/shard_map/pallas_call | solution.py:580
  59.6 2.2 %shard_map.85 = (f32[256,128]{1,0:T(8,128)}, f32[256,128]{1,0:T(8,128)}, f32[3,256]{1,0:T(4,128)}, bf16[1024,2048]{1,0:T(8,128)(2,1)}) custom-call(f32[256,128]{1,0:T(8,128)S(1)} %get-tuple-element.8.refs_0_, f32[256,128]{1,0:T(8,128)S(1)} %get-tuple-element.9.refs_1_, f32[3,256]{1,0:T(4,128)S(1)} %get-tuple-element.10.refs_2_, ...), custom_call_target="tpu_custom_call" | custom-call | tf_op jit(solution)/shard_map/pallas_call | solution.py:624

commit v5 on v4

--- a/solution.py
+++ b/solution.py
@@ -32,6 +32,14 @@
 AROUND = (4, 2, 6, 3, 5, 1, 7, 0)
 
 
+def groups():
+    steps = {t: min(t[0], 4 - t[0]) + min(t[1], 4 - t[1]) for t in OFFSETS}
+    return [[t for t in OFFSETS if low <= steps[t] <= high] for low, high in ((0, 1), (2, 2), (3, 4))]
+
+
+GROUPS = groups()
+
+
 def mm(a, b, dims):
     return lax.dot_general(a, b, dims, preferred_element_type=F32)
 
@@ -45,7 +53,7 @@
     second_ref, resid_ref, coeffs_ref, tile_ref,
     map_ref, kc_ref, coef_ref, e_ref, s_ref,
     scol, ecol, gcol, kbuf, cj, ci, cit, lbuf,
-    wsend, wside, wfull, wlow, whigh, usend, ured,
+    wsend, wside, wnear, wfull, usend, ured,
     zs_send, zs_recv, ab_send, ab_recv, y_send, y_nat, z_send, z_nat, dot_send, dot_recv,
     ssem, rsem, lsem,
 ):
@@ -63,6 +71,7 @@
     is_diag = c == diag_col
     is_near = c == near_col
     first_row = 2 * c
+    away = lax.rem(z - y + 4, 4)
     r_next = lax.rem(r + 1, ROWS)
     r_prev = lax.rem(r + ROWS - 1, ROWS)
     sibling = 2 * z + (1 - k)
@@ -89,14 +98,11 @@
         def _(tr=tr, tc=tc):
             greet(tr, tc)
 
-    for t in OFFSETS:
-        greet(plane_row(t), c_prev)
-        greet(plane_row(t), c_next)
-    for t in range(2, COLS - 1):
+    for t in range(1, COLS):
         greet(r, lax.rem(c + t, COLS))
     greet(r_next, c)
     greet(r_prev, c)
-    pl.semaphore_wait(barrier, 16 + 32 + 5 + 2 - is_diag.astype(jnp.int32))
+    pl.semaphore_wait(barrier, 16 + 7 + 2 - is_diag.astype(jnp.int32))
 
     def remote(src, dst, sem, tr, tc, out=None):
         pltpu.make_async_remote_copy(
@@ -108,14 +114,14 @@
     def local(src, dst, sem):
         pltpu.make_async_copy(src, dst, rsem.at[sem]).start()
 
-    def either(here, src, dst, sem, tr, tc):
+    def either(here, src, dst, sem, tr, tc, out=None):
         @pl.when(here)
         def _():
             local(src, dst, sem)
 
         @pl.when(jnp.logical_not(here))
         def _():
-            remote(src, dst, sem, tr, tc)
+            remote(src, dst, sem, tr, tc, out)
 
     def finish_plain(sem, buf):
         finish.append(lambda: wait_bytes(buf, ssem.at[sem]))
@@ -132,8 +138,8 @@
 
         finish.append(run)
 
-    S, E, K2, CB, AB, YN, ZN, DOT, ZS = range(9)
-    K1, C1, C3, APP = 9, 11, 15, 19
+    E, K2, CB, AB, YN, ZN, DOT, ZS = range(8)
+    K1, C1, C3, S, HW, APP = 8, 10, 14, 18, 22, 24
 
     loads[0].wait()
     loads[1].wait()
@@ -142,9 +148,9 @@
         src = s_ref.at[pl.ds(pl.multiple_of(tr * VS, VS), VS), :]
         dst = scol.at[odd * COLS + c]
         if t == (0, 0):
-            either(is_diag, src, dst, S, tr, diag_col)
+            either(is_diag, src, dst, S + away, tr, diag_col, S)
         else:
-            remote(src, dst, S, tr, diag_col)
+            remote(src, dst, S + away, tr, diag_col, S)
     finish_but_one(is_diag, S, scol, ROWS)
     for t in OFFSETS:
         tr = plane_row(t)
@@ -293,6 +299,27 @@
     def split(v):
         high = v.astype(BF16)
         return high, (v - high.astype(F32)).astype(BF16)
+
+    def restrict_first():
+        acc = [None] * 4
+
+        def add(h, v):
+            acc[h] = v if acc[h] is None else acc[h] + v
+
+        for step in (0, 1, 3, 2):
+            wait_bytes(scol.at[pl.ds(0, 4)], rsem.at[S + step])
+            place_in = lax.rem(z + step, 4)
+            for h in range(2):
+                j = KR * h + place_in
+                value = jnp.concatenate([scol[2 * j], scol[2 * j + 1]], axis=1) * PRESCALE
+                both = jnp.concatenate(split(value), axis=0)
+                flag = map_ref[1, c * FINE + j] == lax.rem(c * 2 + h + 1, ROWS)
+                up = both * flag.astype(F32).astype(BF16)
+                add(1 + h, mm(both, coef_ref[j, 0], NT))
+                side = mm(jnp.concatenate([both - up, up], axis=0), coef_ref[j, 1], NT)
+                add(h, side[:2 * VS])
+                add(2 + h, side[2 * VS:])
+        spread(acc, 0)
 
     def restrict(parts, app):
         acc = [None] * 4
@@ -313,45 +340,49 @@
                 side = mm(jnp.concatenate([both - up, up], axis=0), coef_ref[j, 1], NT)
                 add(home - 1, side[:2 * VS])
                 add(home + 1, side[2 * VS:])
+        spread(acc, app)
+
+    def spread(acc, app):
         acc = [v[:VS] + v[VS:] for v in acc]
-        wsend[app] = jnp.concatenate([acc[1], acc[2]], axis=1).astype(BF16)
+        sem = HW + app
         wside[app, 0] = acc[0].astype(BF16)
         wside[app, 1] = acc[3].astype(BF16)
-        sem = APP + 4 * app
-        for t in OFFSETS:
-            tr = plane_row(t)
-            remote(wside.at[app, 0], whigh.at[app, r], sem, tr, c_prev)
-            remote(wside.at[app, 1], wlow.at[app, r], sem + 1, tr, c_next)
-            if t == (0, 0):
-                local(wsend.at[app], wfull.at[app, r], sem + 2)
-            else:
-                remote(wsend.at[app], wfull.at[app, r], sem + 2, tr, c)
-        finish_plain(sem, whigh.at[app])
-        finish_plain(sem + 1, wlow.at[app])
-        finish_plain(sem + 2, wfull.at[app, pl.ds(0, ROWS - 1)])
+        remote(wside.at[app, 0], wnear.at[app, 1], sem, r, c_prev)
+        remote(wside.at[app, 1], wnear.at[app, 0], sem, r, c_next)
+        finish_plain(sem, wside.at[app])
+        wait_bytes(wnear.at[app], rsem.at[sem])
+        total = [acc[1 + h] + wnear[app, h].astype(F32) for h in range(2)]
+        wsend[app] = jnp.concatenate(total, axis=1).astype(BF16)
+        for g in (2, 1, 0):
+            sem = APP + 4 * app + g
+            for t in GROUPS[g]:
+                if t == (0, 0):
+                    local(wsend.at[app], wfull.at[app, r], sem)
+                else:
+                    remote(wsend.at[app], wfull.at[app, r], sem, plane_row(t), c)
+            finish_plain(sem, wfull.at[app, pl.ds(0, len(GROUPS[g]) - (g == 0))])
 
     def coarse_apply(app):
-        sem = APP + 4 * app
-        wait_bytes(wfull.at[app], rsem.at[sem + 2])
-        wait_bytes(whigh.at[app], rsem.at[sem])
-        wait_bytes(wlow.at[app], rsem.at[sem + 1])
-        full = wfull[app].reshape(NVEC, 2 * BANDS)
-        part = mm(full[:, :BANDS], kc_ref[0, 0], NT) + mm(full[:, BANDS:], kc_ref[0, 1], NT)
-        part = part + mm(wlow[app].reshape(NVEC, BANDS), kc_ref[0, 0], NT)
-        part = part + mm(whigh[app].reshape(NVEC, BANDS), kc_ref[0, 1], NT)
-        usend[app] = part.astype(BF16).reshape(ROWS, VS, BANDS)
-        for t in OFFSETS:
-            tr = plane_row(t)
-            src = usend.at[app, tr]
-            own = ured.at[app, (1 + odd) * COLS + c]
-            near = ured.at[app, 3 * (1 - odd) * COLS + c]
-            if t == (0, 0):
-                either(is_diag, src, own, sem + 3, tr, diag_col)
-                either(is_near, src, near, sem + 3, tr, near_col)
-            else:
-                remote(src, own, sem + 3, tr, diag_col)
-                remote(src, near, sem + 3, tr, near_col)
-        finish_but_one(jnp.logical_or(is_diag, is_near), sem + 3, ured.at[app], 4 * COLS)
+        sem = APP + 4 * app + 3
+        for g, group in enumerate(GROUPS):
+            wait_bytes(wfull.at[app, pl.ds(0, len(group))], rsem.at[APP + 4 * app + g])
+            slots = [plane_row(t) for t in group]
+            own = jnp.concatenate([wfull[app, tr] for tr in slots], axis=0)
+            part = mm(own[:, :BANDS], kc_ref[0, 0], NT) + mm(own[:, BANDS:], kc_ref[0, 1], NT)
+            part = part.astype(BF16)
+            for n, tr in enumerate(slots):
+                usend[app, tr] = part[n * VS:(n + 1) * VS]
+            for t, tr in zip(group, slots):
+                src = usend.at[app, tr]
+                own = ured.at[app, (1 + odd) * COLS + c]
+                near = ured.at[app, 3 * (1 - odd) * COLS + c]
+                if t == (0, 0):
+                    either(is_diag, src, own, sem, tr, diag_col)
+                    either(is_near, src, near, sem, tr, near_col)
+                else:
+                    remote(src, own, sem, tr, diag_col)
+                    remote(src, near, sem, tr, near_col)
+        finish_but_one(jnp.logical_or(is_diag, is_near), sem, ured.at[app], 4 * COLS)
 
     def reduce_coarse(app):
         wait_bytes(ured.at[app], rsem.at[APP + 4 * app + 3])
@@ -434,8 +465,7 @@
             value = mm(lbuf[home, rows], coef_ref[j, 0], NN) + mm(lbuf[other, rows], coef_ref[j, 1], NN)
             tile_ref[rows, pl.ds(j * BANDS, BANDS)] = value.astype(BF16)
 
-    wait_bytes(scol, rsem.at[S])
-    restrict([s_block(j) for j in range(FINE)], 0)
+    restrict_first()
     bulk_second()
     coarse_apply(0)
     bulk_third()
@@ -569,7 +599,7 @@
 def per_device(coarse_kernel, interp_coef, interp_map, energy, start_vectors):
     vmem = pl.BlockSpec(memory_space=pltpu.VMEM)
     hbm = pl.BlockSpec(memory_space=pltpu.HBM)
-    nsem = 19 + 8
+    nsem = 24 + 8
     shapes = (
         jax.ShapeDtypeStruct((NVEC, HALF), F32),
         jax.ShapeDtypeStruct((NVEC, HALF), F32),
@@ -598,9 +628,8 @@
             pltpu.VMEM((4, KR * BANDS, BANDS), BF16),
             pltpu.VMEM((2, VS, 2 * BANDS), BF16),
             pltpu.VMEM((2, 2, VS, BANDS), BF16),
+            pltpu.VMEM((2, 2, VS, BANDS), BF16),
             pltpu.VMEM((2, ROWS, VS, 2 * BANDS), BF16),
-            pltpu.VMEM((2, ROWS, VS, BANDS), BF16),
-            pltpu.VMEM((2, ROWS, VS, BANDS), BF16),
             pltpu.VMEM((2, ROWS, VS, BANDS), BF16),
             pltpu.VMEM((2, 4 * COLS, VS, BANDS), BF16),
             pltpu.VMEM((3, 1, HALF), F32),

time: 61.9 us -> 58.8 us (0.950)
  Pallas kernels: 61.2 us -> 58 us
    pallas_call x1, Pallas kernels: 59 us -> 55.9 us  [per_device(): pl.pallas_call(kernel, out_shape=shapes, in_specs=[hbm] * 5, out_specs=(v...]
where the time goes in v5:
time: 58.8 us; the launch traced here: 58.7 us
  Pallas kernels  58 us (99%)
  between operations  0.64 us (1%)
    pallas_call x1, Pallas kernels, per_device(): pl.pallas_call(kernel, out_shape=shapes, in_specs=[hbm] * 5, out_specs=(v...  55.9 us
    pallas_call x1, Pallas kernels, per_device(): pl.pallas_call(write_out, out_shape=shapes, in_specs=[vmem] * 4, out_spec...  2.19 us

profile of v5, /device:TPU:1, one launch (start us, length us, event | category | flops | bytes accessed | tf_op | source)
XLA Modules:
  0.0 58.7 jit_solution(10590111095513859481)
XLA Ops:
  0.6 55.9 %shard_map.84 = (f32[256,128]{1,0:T(8,128)S(1)}, f32[256,128]{1,0:T(8,128)S(1)}, f32[3,256]{1,0:T(4,128)S(1)}, bf16[1024,2048]{1,0:T(8,128)(2,1)S(1)}) custom-call(s32[2,64]{1,0:T(2,128)} %bitcast.2, bf16[1,2,256,256]{3,2,1,0:T(8,128)(2,1)} %kc_hbm.1, bf16[8,2,256,256]{3,2,1,0:T(8,128)(2,1)} %coef_hbm.1, f32[1,128]{1,0:T(1,128)} %bitcast.3, f32[256,128]{1,0:T(8,128)} %s_hbm.1), custom_call_target="tpu_custom_call" | custom-call | tf_op jit(solution)/shard_map/pallas_call | solution.py:610
  56.5 2.2 %shard_map.85 = (f32[256,128]{1,0:T(8,128)}, f32[256,128]{1,0:T(8,128)}, f32[3,256]{1,0:T(4,128)}, bf16[1024,2048]{1,0:T(8,128)(2,1)}) custom-call(f32[256,128]{1,0:T(8,128)S(1)} %get-tuple-element.8.refs_0_, f32[256,128]{1,0:T(8,128)S(1)} %get-tuple-element.9.refs_1_, f32[3,256]{1,0:T(4,128)S(1)} %get-tuple-element.10.refs_2_, ...), custom_call_target="tpu_custom_call" | custom-call | tf_op jit(solution)/shard_map/pallas_call | solution.py:653

commit v6 on v5

--- a/solution.py
+++ b/solution.py
@@ -52,9 +52,9 @@
     map_hbm, kc_hbm, coef_hbm, e_hbm, s_hbm,
     second_ref, resid_ref, coeffs_ref, tile_ref,
     map_ref, kc_ref, coef_ref, e_ref, s_ref,
-    scol, ecol, gcol, kbuf, cj, ci, cit, lbuf,
+    scol, ecol, kbuf, cj, ci, cit, lbuf,
     wsend, wside, wnear, wfull, usend, ured,
-    zs_send, zs_recv, ab_send, ab_recv, y_send, y_nat, z_send, z_nat, dot_send, dot_recv,
+    zs_send, zs_recv, ab_send, ab_recv, y_send, y_nat, zred, wdot, usum, uside, z_send, z_nat, dot_send, dot_recv,
     ssem, rsem, lsem,
 ):
     r = lax.axis_index("row")
@@ -138,8 +138,8 @@
 
         finish.append(run)
 
-    E, K2, CB, AB, YN, ZN, DOT, ZS = range(8)
-    K1, C1, C3, S, HW, APP = 8, 10, 14, 18, 22, 24
+    E, K2, CB, AB, YN, WD, UN, ZN, DOT, ZS = range(10)
+    K1, C1, C3, S, HW, APP = 10, 12, 16, 20, 24, 26
 
     loads[0].wait()
     loads[1].wait()
@@ -374,23 +374,30 @@
                 usend[app, tr] = part[n * VS:(n + 1) * VS]
             for t, tr in zip(group, slots):
                 src = usend.at[app, tr]
-                own = ured.at[app, (1 + odd) * COLS + c]
-                near = ured.at[app, 3 * (1 - odd) * COLS + c]
+                if app:
+                    half = lax.div(tr, 2)
+                    either(half == c, src, zred.at[c, lax.rem(tr, 2)], sem, r, half)
+                    continue
+                own = ured.at[(1 + odd) * COLS + c]
+                near = ured.at[3 * (1 - odd) * COLS + c]
                 if t == (0, 0):
                     either(is_diag, src, own, sem, tr, diag_col)
                     either(is_near, src, near, sem, tr, near_col)
                 else:
                     remote(src, own, sem, tr, diag_col)
                     remote(src, near, sem, tr, near_col)
-        finish_but_one(jnp.logical_or(is_diag, is_near), sem, ured.at[app], 4 * COLS)
-
-    def reduce_coarse(app):
-        wait_bytes(ured.at[app], rsem.at[APP + 4 * app + 3])
+        if app:
+            finish_plain(sem, usend.at[app, pl.ds(0, ROWS - 2)])
+        else:
+            finish_but_one(jnp.logical_or(is_diag, is_near), sem, ured, 4 * COLS)
+
+    def reduce_coarse():
+        wait_bytes(ured, rsem.at[APP + 3])
         u = []
         for h in range(4):
-            total = ured[app, h * COLS].astype(F32)
+            total = ured[h * COLS].astype(F32)
             for t in range(1, COLS):
-                total = total + ured[app, h * COLS + t].astype(F32)
+                total = total + ured[h * COLS + t].astype(F32)
             u.append(jnp.concatenate(split(total), axis=0))
         return u
 
@@ -426,6 +433,11 @@
 
     own_place = place(lax.rem(r, 8))
 
+    lane_group = lax.div(lax.broadcasted_iota(jnp.int32, (1, HALF), 1), VS)
+
+    def place_row(shift):
+        return lane_group == shift
+
     def as_row(v):
         return jnp.sum(jnp.where(own_place, v, 0.0), axis=0, keepdims=True)
 
@@ -469,23 +481,27 @@
     bulk_second()
     coarse_apply(0)
     bulk_third()
-    u = reduce_coarse(0)
+    u = reduce_coarse()
     wait_bytes(ecol, rsem.at[E])
     parts = []
-    ss = sg = gg = jnp.zeros((VS, 1), F32)
+    ss = sg = gg = gdg = jnp.zeros((VS, 1), F32)
     for j in range(FINE):
         s_j = s_block(j)
         y_j = prolong(u, j)
         g_j = y_j + d_block(j) * s_j
-        gcol[j] = g_j
         parts.append(g_j)
         keep(y_send, j, y_j)
         ss = ss + row_sum(s_j * s_j)
         sg = sg + row_sum(s_j * g_j)
         gg = gg + row_sum(g_j * g_j)
+        gdg = gdg + row_sum(g_j * g_j * d_block(j))
 
     restrict(parts, 1)
-    for n, v in enumerate((ss, sg, gg)):
+    for h in range(2):
+        src = wsend.at[1, :, pl.ds(h * BANDS, BANDS)]
+        either(jnp.logical_and(is_diag, odd == h), src, wdot.at[odd], WD, first_row + h, diag_col)
+    finish_but_one(is_diag, WD, wdot, 2)
+    for n, v in enumerate((ss, sg, gg, gdg)):
         zs_send[n] = as_row(v)
     local(zs_send, zs_recv.at[c], ZS)
     for t in range(1, COLS):
@@ -498,7 +514,7 @@
     for t in range(1, COLS):
         mean = mean + zs_recv[t]
     mean = mean / ORDER
-    ss, sg, gg = (as_column(mean[n], own_place) for n in range(3))
+    ss, sg, gg, gdg = (as_column(mean[n], own_place) for n in range(4))
     var = ss + EPS * PRESCALE * PRESCALE
     scale = jnp.sqrt(var)
     alpha_one = (sg + SHIFT * ss) / var
@@ -507,7 +523,10 @@
     beta = jnp.sqrt(jnp.maximum(remain_sq, 0.0) + EPS)
     inv = 1.0 / (scale * beta)
     over = beta / scale
-    for n, v in enumerate((alpha_one, beta, inv, over)):
+    sec_sec = (gg + 2.0 * mix * sg + mix * mix * ss) * inv * inv
+    known = (gdg + 2.0 * mix * gg + mix * mix * sg) * inv * inv + SHIFT * sec_sec
+    known = known - over * inv * (sg + mix * ss)
+    for n, v in enumerate((alpha_one, beta, inv, over, known)):
         ab_send[n] = as_row(v)
     coarse_apply(1)
     for t in OFFSETS:
@@ -518,18 +537,24 @@
     finish_plain(AB, ab_recv.at[pl.ds(0, ROWS - 1)])
     to_native(y_send, y_nat, YN)
     bulk_siblings()
-    u = reduce_coarse(1)
-    dot = jnp.zeros((VS, 1), F32)
-    for j in range(FINE):
-        s_j = s_block(j)
-        g_j = gcol[j]
-        z_j = prolong(u, j)
-        h_j = z_j + d_block(j) * g_j
-        sec = (g_j + mix * s_j) * inv
-        shifted = (h_j + mix * g_j) * inv + SHIFT * sec - over * s_j
-        dot = dot + row_sum(sec * shifted)
-        keep(z_send, j, z_j)
-    dot_send[...] = as_row(dot)
+
+    wait_bytes(zred, rsem.at[APP + 7])
+    wait_bytes(wdot, rsem.at[WD])
+    line, own_u = None, []
+    for h in range(2):
+        total = zred[0, h].astype(F32)
+        for t in range(1, COLS):
+            total = total + zred[t, h].astype(F32)
+        own_u.append(total)
+        usum[pl.ds(h * VS, VS), :] = total.astype(BF16)
+        inner = row_sum(total * wdot[h].astype(F32))
+        row = jnp.sum(jnp.where(place(2 * lax.rem(c, 4) + h), inner, 0.0), axis=0, keepdims=True)
+        line = row if line is None else line + row
+    remote(usum, uside.at[0], UN, r_next, c)
+    remote(usum, uside.at[1], UN, r_prev, c)
+    finish_plain(UN, uside)
+    own_u = jnp.concatenate(split(jnp.concatenate(own_u, axis=0)), axis=0)
+    dot_send[...] = line
     for tz in AROUND:
         for t in OFFSETS:
             if t == (0, 0) and tz == 0:
@@ -537,9 +562,29 @@
             else:
                 remote(dot_send, dot_recv.at[c * ROWS + r], DOT, plane_row(t), lax.rem(c + tz, COLS))
     finish_plain(DOT, dot_recv.at[pl.ds(0, ROWS * COLS - 1)])
-    to_native(z_send, z_nat, ZN)
     bulk_wait()
     left_part()
+
+    wait_bytes(uside, rsem.at[UN])
+    for i in range(KR):
+        if i == 0:
+            side = uside[0]
+        elif i == KR - 1:
+            side = uside[1]
+        else:
+            up = (map_ref[1, r * KR + i] == r_next).astype(F32)
+            side = uside[0] * (1.0 - up).astype(BF16) + uside[1] * up.astype(BF16)
+        value = mm(own_u, ci[i, 0], NN)
+        value = value[:2 * VS] + value[2 * VS:] + mm(side, ci[i, 1], NN)
+        for h in range(2):
+            z_send[2 * i + h] = value[:, h * HALF:(h + 1) * HALF].astype(BF16)
+    for tz in AROUND:
+        tc = lax.rem(c + tz, COLS)
+        if tz == 0:
+            local(z_send.at[tc], z_nat.at[c], ZN)
+        else:
+            remote(z_send.at[tc], z_nat.at[c], ZN, r, tc)
+    finish_plain(ZN, z_send.at[pl.ds(0, COLS - 1)])
     for j in range(FINE):
         tile_piece(j)
 
@@ -557,11 +602,21 @@
         sec = (image + mix_i * first) * inv_i
         second_ref[rows, :] = sec
         resid_ref[rows, :] = (diag * image + mix_i * image) * inv_i + SHIFT * sec - over_i * first
+    wait_bytes(z_nat, rsem.at[ZN])
+    image_two = z_nat[...].reshape(NVEC, HALF).astype(F32)
     wait_bytes(dot_recv, rsem.at[DOT])
-    total = dot_recv[pl.ds(0, ROWS)]
-    for t in range(1, COLS):
-        total = total + dot_recv[pl.ds(t * ROWS, ROWS)]
-    alpha_two = total / ORDER
+    inner = []
+    for h in range(2):
+        total = dot_recv[h * 4 * ROWS]
+        for t in range(1, 4 * ROWS):
+            total = total + dot_recv[h * 4 * ROWS + t]
+        inner.append(total / ORDER)
+
+    def second_alpha(i):
+        inv_row = ab_recv[i, 2]
+        return ab_recv[i, 4] + jnp.where(place_row(i % 8), inner[i // 8], 0.0) * inv_row * inv_row
+
+    alpha_two = [second_alpha(i) for i in range(ROWS)]
     lines = []
     for get in (lambda i: ab_recv[i, 0], lambda i: ab_recv[i, 1], lambda i: alpha_two[i]):
         halves = []
@@ -572,13 +627,12 @@
             halves.append(value)
         lines.append(jnp.concatenate(halves, axis=1))
     coeffs_ref[...] = jnp.concatenate(lines, axis=0)
-    wait_bytes(z_nat, rsem.at[ZN])
     for i in range(ROWS):
         rows = pl.ds(i * VS, VS)
         mask = place(i % 8)
         column = as_column(alpha_two[i], mask)
         inv_i = as_column(ab_recv[i, 2], mask)
-        resid_ref[rows, :] = resid_ref[rows, :] + z_nat[i].astype(F32) * inv_i - column * second_ref[rows, :]
+        resid_ref[rows, :] = resid_ref[rows, :] + image_two[i * VS:(i + 1) * VS] * inv_i - column * second_ref[rows, :]
 
     for run in finish:
         run()
@@ -599,7 +653,7 @@
 def per_device(coarse_kernel, interp_coef, interp_map, energy, start_vectors):
     vmem = pl.BlockSpec(memory_space=pltpu.VMEM)
     hbm = pl.BlockSpec(memory_space=pltpu.HBM)
-    nsem = 24 + 8
+    nsem = 26 + 8
     shapes = (
         jax.ShapeDtypeStruct((NVEC, HALF), F32),
         jax.ShapeDtypeStruct((NVEC, HALF), F32),
@@ -620,7 +674,6 @@
             pltpu.VMEM((NVEC, HALF), F32),
             pltpu.VMEM((16, VS, HALF), F32),
             pltpu.VMEM((16, 1, HALF), F32),
-            pltpu.VMEM((FINE, VS, BANDS), F32),
             pltpu.VMEM((12, BANDS, BANDS), BF16),
             pltpu.VMEM((4, 2, BANDS, BANDS), BF16),
             pltpu.VMEM((KR, 2, BANDS, BANDS), BF16),
@@ -631,15 +684,19 @@
             pltpu.VMEM((2, 2, VS, BANDS), BF16),
             pltpu.VMEM((2, ROWS, VS, 2 * BANDS), BF16),
             pltpu.VMEM((2, ROWS, VS, BANDS), BF16),
-            pltpu.VMEM((2, 4 * COLS, VS, BANDS), BF16),
-            pltpu.VMEM((3, 1, HALF), F32),
-            pltpu.VMEM((COLS, 3, 1, HALF), F32),
+            pltpu.VMEM((4 * COLS, VS, BANDS), BF16),
             pltpu.VMEM((4, 1, HALF), F32),
-            pltpu.VMEM((ROWS, 4, 1, HALF), F32),
+            pltpu.VMEM((COLS, 4, 1, HALF), F32),
+            pltpu.VMEM((5, 1, HALF), F32),
+            pltpu.VMEM((ROWS, 5, 1, HALF), F32),
             pltpu.VMEM((16, VS, HALF), BF16),
             pltpu.VMEM((16, VS, HALF), BF16),
-            pltpu.VMEM((16, VS, HALF), BF16),
-            pltpu.VMEM((16, VS, HALF), BF16),
+            pltpu.VMEM((COLS, 2, VS, BANDS), BF16),
+            pltpu.VMEM((2, VS, BANDS), BF16),
+            pltpu.VMEM((2 * VS, BANDS), BF16),
+            pltpu.VMEM((2, 2 * VS, BANDS), BF16),
+            pltpu.VMEM((COLS, 2 * VS, HALF), BF16),
+            pltpu.VMEM((COLS, 2 * VS, HALF), BF16),
             pltpu.VMEM((1, HALF), F32),
             pltpu.VMEM((COLS * ROWS, 1, HALF), F32),
             pltpu.SemaphoreType.DMA((nsem,)),

time: 58.8 us -> 58.1 us (0.988)
  Pallas kernels: 58 us -> 57.4 us
    pallas_call x1, Pallas kernels: 55.9 us -> 55.2 us  [per_device(): pl.pallas_call(kernel, out_shape=shapes, in_specs=[hbm] * 5, out_specs=(v...]
where the time goes in v6:
time: 58.1 us; the launch traced here: 58 us
  Pallas kernels  57.4 us (99%)
  between operations  0.64 us (1%)
    pallas_call x1, Pallas kernels, per_device(): pl.pallas_call(kernel, out_shape=shapes, in_specs=[hbm] * 5, out_specs=(v...  55.2 us
    pallas_call x1, Pallas kernels, per_device(): pl.pallas_call(write_out, out_shape=shapes, in_specs=[vmem] * 4, out_spec...  2.19 us

profile of v6, /device:TPU:1, one launch (start us, length us, event | category | flops | bytes accessed | tf_op | source)
XLA Modules:
  0.0 58.0 jit_solution(2978680915040820187)
XLA Ops:
  0.6 55.2 %shard_map.84 = (f32[256,128]{1,0:T(8,128)S(1)}, f32[256,128]{1,0:T(8,128)S(1)}, f32[3,256]{1,0:T(4,128)S(1)}, bf16[1024,2048]{1,0:T(8,128)(2,1)S(1)}) custom-call(s32[2,64]{1,0:T(2,128)} %bitcast.2, bf16[1,2,256,256]{3,2,1,0:T(8,128)(2,1)} %kc_hbm.1, bf16[8,2,256,256]{3,2,1,0:T(8,128)(2,1)} %coef_hbm.1, f32[1,128]{1,0:T(1,128)} %bitcast.3, f32[256,128]{1,0:T(8,128)} %s_hbm.1), custom_call_target="tpu_custom_call" | custom-call | tf_op jit(solution)/shard_map/pallas_call | solution.py:664
  55.8 2.2 %shard_map.85 = (f32[256,128]{1,0:T(8,128)}, f32[256,128]{1,0:T(8,128)}, f32[3,256]{1,0:T(4,128)}, bf16[1024,2048]{1,0:T(8,128)(2,1)}) custom-call(f32[256,128]{1,0:T(8,128)S(1)} %get-tuple-element.8.refs_0_, f32[256,128]{1,0:T(8,128)S(1)} %get-tuple-element.9.refs_1_, f32[3,256]{1,0:T(4,128)S(1)} %get-tuple-element.10.refs_2_, ...), custom_call_target="tpu_custom_call" | custom-call | tf_op jit(solution)/shard_map/pallas_call | solution.py:710

commit v7 on v6

--- a/solution.py
+++ b/solution.py
@@ -190,8 +190,6 @@
                 remote(kbuf.at[4 * slot + 2], kbuf.at[4 * slot], K2, r, c_next)
 
     def bulk_first():
-        row_blocks(0)
-
         @pl.when(serves)
         def _():
             for t in (1, 3):
@@ -308,6 +306,8 @@
 
         for step in (0, 1, 3, 2):
             wait_bytes(scol.at[pl.ds(0, 4)], rsem.at[S + step])
+            if step == 0:
+                row_blocks(0)
             place_in = lax.rem(z + step, 4)
             for h in range(2):
                 j = KR * h + place_in
@@ -528,6 +528,7 @@
     known = known - over * inv * (sg + mix * ss)
     for n, v in enumerate((alpha_one, beta, inv, over, known)):
         ab_send[n] = as_row(v)
+    bulk_siblings()
     coarse_apply(1)
     for t in OFFSETS:
         if t == (0, 0):
@@ -536,7 +537,8 @@
             remote(ab_send, ab_recv.at[r], AB, plane_row(t), c)
     finish_plain(AB, ab_recv.at[pl.ds(0, ROWS - 1)])
     to_native(y_send, y_nat, YN)
-    bulk_siblings()
+    bulk_wait()
+    left_part()
 
     wait_bytes(zred, rsem.at[APP + 7])
     wait_bytes(wdot, rsem.at[WD])
@@ -562,9 +564,9 @@
             else:
                 remote(dot_send, dot_recv.at[c * ROWS + r], DOT, plane_row(t), lax.rem(c + tz, COLS))
     finish_plain(DOT, dot_recv.at[pl.ds(0, ROWS * COLS - 1)])
-    bulk_wait()
-    left_part()
-
+
+    for j in range(4):
+        tile_piece(j)
     wait_bytes(uside, rsem.at[UN])
     for i in range(KR):
         if i == 0:
@@ -585,7 +587,7 @@
         else:
             remote(z_send.at[tc], z_nat.at[c], ZN, r, tc)
     finish_plain(ZN, z_send.at[pl.ds(0, COLS - 1)])
-    for j in range(FINE):
+    for j in range(4, FINE):
         tile_piece(j)
 
     wait_bytes(y_nat, rsem.at[YN])

time: 58.1 us -> 56.4 us (0.971)
  Pallas kernels: 57.4 us -> 55.6 us
    pallas_call x1, Pallas kernels: 55.2 us -> 53.4 us  [per_device(): pl.pallas_call(kernel, out_shape=shapes, in_specs=[hbm] * 5, out_specs=(v...]
where the time goes in v7:
time: 56.4 us; the launch traced here: 56.3 us
  Pallas kernels  55.6 us (99%)
  between operations  0.64 us (1%)
    pallas_call x1, Pallas kernels, per_device(): pl.pallas_call(kernel, out_shape=shapes, in_specs=[hbm] * 5, out_specs=(v...  53.4 us
    pallas_call x1, Pallas kernels, per_device(): pl.pallas_call(write_out, out_shape=shapes, in_specs=[vmem] * 4, out_spec...  2.19 us

profile of v7, /device:TPU:1, one launch (start us, length us, event | category | flops | bytes accessed | tf_op | source)
XLA Modules:
  0.0 56.3 jit_solution(13209968902786382298)
XLA Ops:
  0.6 53.4 %shard_map.84 = (f32[256,128]{1,0:T(8,128)S(1)}, f32[256,128]{1,0:T(8,128)S(1)}, f32[3,256]{1,0:T(4,128)S(1)}, bf16[1024,2048]{1,0:T(8,128)(2,1)S(1)}) custom-call(s32[2,64]{1,0:T(2,128)} %bitcast.2, bf16[1,2,256,256]{3,2,1,0:T(8,128)(2,1)} %kc_hbm.1, bf16[8,2,256,256]{3,2,1,0:T(8,128)(2,1)} %coef_hbm.1, f32[1,128]{1,0:T(1,128)} %bitcast.3, f32[256,128]{1,0:T(8,128)} %s_hbm.1), custom_call_target="tpu_custom_call" | custom-call | tf_op jit(solution)/shard_map/pallas_call | solution.py:666
  54.1 2.2 %shard_map.85 = (f32[256,128]{1,0:T(8,128)}, f32[256,128]{1,0:T(8,128)}, f32[3,256]{1,0:T(4,128)}, bf16[1024,2048]{1,0:T(8,128)(2,1)}) custom-call(f32[256,128]{1,0:T(8,128)S(1)} %get-tuple-element.8.refs_0_, f32[256,128]{1,0:T(8,128)S(1)} %get-tuple-element.9.refs_1_, f32[3,256]{1,0:T(4,128)S(1)} %get-tuple-element.10.refs_2_, ...), custom_call_target="tpu_custom_call" | custom-call | tf_op jit(solution)/shard_map/pallas_call | solution.py:712
